TPU v7x, 32 devices: a whole 2x2x4 slice. The times are simulated.
32 devices in a mesh: shard: 4 (over y, core), seq: 8 (over z, x).
Axes of the slice: x: 2, y: 2, z: 4, core: 2. Of those that a mesh axis runs over, the one named last changes fastest.
Arguments:
- tokens: bfloat16 [2, 4, 4096, 1024], P(None, 'shard', 'seq'), may hold values from -6 to 6
- cotangent: bfloat16 [2, 4, 4096, 1024], P(None, 'shard', 'seq'), may hold values from -6 to 6
- lengths: int32 [2, 4], P(None, 'shard'), may hold values from 1024 to 4096
- variates: int32 [2, 4, 4096], P(None, 'shard', 'seq'), may hold values from 0 to 7
- positions: int32 [2, 4, 4096], P(None, 'shard', 'seq'), may hold values from 0 to 4095
- attn_gain: float32 [1024], replicated, may hold values from 0.5 to 1.5
- w_query: bfloat16 [1024, 1024], P('shard'), may hold values from -0.1875 to 0.1875
- w_key: bfloat16 [1024, 1024], P('shard'), may hold values from -0.1875 to 0.1875
- w_value: bfloat16 [1024, 1024], P('shard'), may hold values from -0.1875 to 0.1875
- w_out: bfloat16 [1024, 1024], P('shard'), may hold values from -2 to 2
- bias_table: float32 [16, 2], replicated, may hold values from -3 to 3
- ffn_gain: float32 [1024], replicated, may hold values from 0.5 to 1.5
- w_gate: bfloat16 [1024, 4096], P('shard'), may hold values from -0.1875 to 0.1875
- w_up: bfloat16 [1024, 4096], P('shard'), may hold values from -0.1875 to 0.1875
- w_down: bfloat16 [4096, 1024], P('shard'), may hold values from -0.09375 to 0.09375
Outputs:
- output: bfloat16 [2, 4, 4096, 1024], P(None, 'shard', 'seq')
- grad_tokens: bfloat16 [2, 4, 4096, 1024], P(None, 'shard', 'seq')
- grad_attn_gain: float32 [1024], replicated
- grad_query: float32 [1024, 1024], P(('shard', 'seq'))
- grad_key: float32 [1024, 1024], P(('shard', 'seq'))
- grad_value: float32 [1024, 1024], P(('shard', 'seq'))
- grad_out: float32 [1024, 1024], P(('shard', 'seq'))
- grad_bias: float32 [16, 2], replicated
- grad_ffn_gain: float32 [1024], replicated
- grad_gate: float32 [1024, 4096], P(('shard', 'seq'))
- grad_up: float32 [1024, 4096], P(('shard', 'seq'))
- grad_down: float32 [4096, 1024], P(('shard', 'seq'))
All inputs are finite; a program needn't handle non-finite values.
Results may differ from a plain program's by a relative error of at most 0.015.
Values may be sent and summed in bfloat16 or wider, within the bound.
A program may use at most 448 MiB of HBM per device.

v0:
```python
import math

import jax
import jax.numpy as jnp
from jax import lax
from jax.sharding import PartitionSpec as P

EPSILON = 1e-06
MASKED_SCORE = -1000000000.0
ROTARY_BASE = 10000.0


def rotary_tables(places, half_dim):
    frequency = jnp.exp(-math.log(ROTARY_BASE) * jnp.arange(half_dim, dtype=jnp.float32) / half_dim)
    angles = places.astype(jnp.float32)[..., None, :] * frequency[:, None]
    return (jnp.cos(angles), jnp.sin(angles))


def rotate_cols(values, cosine, sine_table, reverse):
    half_dim = values.shape[-2] // 2
    first_half = values[..., :half_dim, :]
    second_half = values[..., half_dim:, :]
    if reverse:
        return jnp.concatenate(
            [
                first_half * cosine + second_half * sine_table,
                second_half * cosine - first_half * sine_table,
            ],
            axis=-2,
        )
    return jnp.concatenate(
        [
            first_half * cosine - second_half * sine_table,
            second_half * cosine + first_half * sine_table,
        ],
        axis=-2,
    )


def block_scores(
    query_block, variate_block, keys_all, variate_row, key_mask, bias_local, scale_factor
):
    scores = (
        jnp.einsum("hdq,hdk->hqk", query_block, keys_all, preferred_element_type=jnp.float32)
        * scale_factor
    )
    same_var = variate_block[:, None] == variate_row[None, :]
    biased = scores + jnp.where(
        same_var[None], bias_local[:, 1][:, None, None], bias_local[:, 0][:, None, None]
    )
    return (jnp.where(key_mask[None, None, :], biased, MASKED_SCORE), same_var)


def split_blocks(values, count_blocks, block_rows):
    lead = values.shape[:-1]
    return jnp.moveaxis(values.reshape(lead + (count_blocks, block_rows)), -2, 0)


def attend_forward(queries, keys_all, values_all, variate_row, length, bias_local):
    local_heads, head_dim, seq_len = queries.shape
    block_rows = min(512, seq_len)
    count_blocks = seq_len // block_rows
    scale_factor = 1.0 / math.sqrt(head_dim)
    key_mask = jnp.arange(seq_len, dtype=jnp.int32) < length

    def one_block(inputs):
        query_block, variate_block = inputs
        masked, same_var = block_scores(
            query_block, variate_block, keys_all, variate_row, key_mask, bias_local, scale_factor
        )
        peak = jnp.max(masked, axis=-1, keepdims=True)
        weights_exp = jnp.exp(masked - peak)
        total = jnp.sum(weights_exp, axis=-1, keepdims=True)
        probs = (weights_exp / total).astype(jnp.bfloat16)
        mixed = jnp.einsum("hqk,hdk->hdq", probs, values_all, preferred_element_type=jnp.float32)
        return (mixed.astype(jnp.bfloat16), peak[..., 0] + jnp.log(total[..., 0]))

    mixed_blocks, log_totals = lax.map(
        one_block,
        (
            split_blocks(queries, count_blocks, block_rows),
            variate_row.reshape(count_blocks, block_rows),
        ),
    )
    mixed = jnp.moveaxis(mixed_blocks, 0, 2).reshape(local_heads, head_dim, seq_len)
    return (mixed, log_totals)


def attend_backward(
    queries,
    keys_all,
    values_all,
    grad_mixed,
    variate_row,
    place_row,
    length,
    log_totals,
    bias_local,
):
    local_heads, head_dim, seq_len = queries.shape
    block_rows = min(512, seq_len)
    count_blocks = seq_len // block_rows
    scale_factor = 1.0 / math.sqrt(head_dim)
    key_mask = jnp.arange(seq_len, dtype=jnp.int32) < length

    def one_block(carry, inputs):
        grad_keys, grad_values, grad_bias = carry
        query_block, grad_block, variate_block, log_block = inputs
        masked, same_var = block_scores(
            query_block, variate_block, keys_all, variate_row, key_mask, bias_local, scale_factor
        )
        probs = jnp.exp(masked - log_block[..., None])
        probs_low = probs.astype(jnp.bfloat16)
        grad_probs = jnp.einsum(
            "hdq,hdk->hqk", grad_block, values_all, preferred_element_type=jnp.float32
        )
        grad_scores = probs * (grad_probs - jnp.sum(probs * grad_probs, axis=-1, keepdims=True))
        grad_low = grad_scores.astype(jnp.bfloat16)
        grad_query = (
            jnp.einsum("hqk,hdk->hdq", grad_low, keys_all, preferred_element_type=jnp.float32)
            * scale_factor
        )
        grad_keys = (
            grad_keys
            + jnp.einsum("hqk,hdq->hdk", grad_low, query_block, preferred_element_type=jnp.float32)
            * scale_factor
        )
        grad_values = grad_values + jnp.einsum(
            "hqk,hdq->hdk", probs_low, grad_block, preferred_element_type=jnp.float32
        )
        grad_wide = grad_low.astype(jnp.float32)
        same_total = jnp.sum(jnp.where(same_var[None], grad_wide, 0.0), axis=(1, 2))
        all_total = jnp.sum(grad_wide, axis=(1, 2))
        grad_bias = grad_bias + jnp.stack([all_total - same_total, same_total], axis=-1)
        return ((grad_keys, grad_values, grad_bias), grad_query)

    start_state = (
        jnp.zeros((local_heads, head_dim, seq_len), jnp.float32),
        jnp.zeros((local_heads, head_dim, seq_len), jnp.float32),
        jnp.zeros((local_heads, 2), jnp.float32),
    )
    (grad_keys, grad_values, grad_bias), query_grads = lax.scan(
        one_block,
        start_state,
        (
            split_blocks(queries, count_blocks, block_rows),
            split_blocks(grad_mixed, count_blocks, block_rows),
            variate_row.reshape(count_blocks, block_rows),
            log_totals,
        ),
    )
    grad_queries = jnp.moveaxis(query_grads, 0, 2).reshape(local_heads, head_dim, seq_len)
    cosine, sine_table = rotary_tables(place_row, head_dim // 2)
    grad_query_pre = rotate_cols(grad_queries, cosine, sine_table, True).astype(jnp.bfloat16)
    grad_key_pre = rotate_cols(grad_keys, cosine, sine_table, True).astype(jnp.bfloat16)
    return (grad_query_pre, grad_key_pre, grad_values.astype(jnp.bfloat16), grad_bias)


def norm_back(grad_normed, inputs_wide, inverse, gain):
    scaled = grad_normed * gain
    grad_inputs = inverse * scaled - inputs_wide * (inverse * inverse * inverse) * jnp.mean(
        scaled * inputs_wide, axis=-1, keepdims=True
    )
    grad_gain = jnp.sum(grad_normed * inputs_wide * inverse, axis=(0, 1))
    return (grad_inputs, grad_gain)


def feature_terms(stored):
    (
        normed_attn,
        mixed_tok,
        normed_ffn,
        grad_q_tok,
        grad_k_tok,
        grad_v_tok,
        grad_attn,
        grad_gate_act,
        grad_up_act,
        hidden,
        grad_ffn,
    ) = stored
    term_query = jnp.einsum(
        "stc,set->ce", normed_attn, grad_q_tok, preferred_element_type=jnp.float32
    )
    term_key = jnp.einsum(
        "stc,set->ce", normed_attn, grad_k_tok, preferred_element_type=jnp.float32
    )
    term_value = jnp.einsum(
        "stc,set->ce", normed_attn, grad_v_tok, preferred_element_type=jnp.float32
    )
    term_out = jnp.einsum("sct,ste->ce", mixed_tok, grad_attn, preferred_element_type=jnp.float32)
    term_gate = jnp.einsum(
        "stc,stf->cf", normed_ffn, grad_gate_act, preferred_element_type=jnp.float32
    )
    term_up = jnp.einsum("stc,stf->cf", normed_ffn, grad_up_act, preferred_element_type=jnp.float32)
    return jnp.concatenate([term_query, term_key, term_value, term_out, term_gate, term_up], axis=1)


def hidden_terms(stored):
    hidden = stored[9]
    grad_ffn = stored[10]
    return jnp.einsum("stc,std->cd", hidden, grad_ffn, preferred_element_type=jnp.float32)


def add_trees(first, second):
    if first is None:
        return second
    return jax.tree.map(jnp.add, first, second)


def on_device(
    tokens,
    cotangent,
    lengths,
    variates,
    positions,
    attn_gain,
    w_query,
    w_key,
    w_value,
    w_out,
    bias_table,
    ffn_gain,
    w_gate,
    w_up,
    w_down,
):
    micro, seq_count, local_len, width = tokens.shape
    heads = bias_table.shape[0]
    head_dim = width // heads
    ffn_width = w_gate.shape[1]
    seq_devices = lax.axis_size("seq")
    local_heads = heads // seq_devices
    seq_index = lax.axis_index("seq")
    bias_local = lax.dynamic_slice_in_dim(bias_table, seq_index * local_heads, local_heads, 0)
    variates_full, places_full = (
        lax.all_gather(variates, "seq", axis=2, tiled=True),
        lax.all_gather(positions, "seq", axis=2, tiled=True),
    )
    cosine_tok, sine_tok = rotary_tables(positions, head_dim // 2)
    row_index = seq_index * local_len + jnp.arange(local_len, dtype=jnp.int32)
    attend_many = jax.vmap(attend_forward, in_axes=(0, 0, 0, 0, 0, None))
    backward_many = jax.vmap(attend_backward, in_axes=(0, 0, 0, 0, 0, 0, 0, 0, None))

    def gather_attn():
        return (
            lax.all_gather(w_query, "shard", axis=0, tiled=True),
            lax.all_gather(w_key, "shard", axis=0, tiled=True),
            lax.all_gather(w_value, "shard", axis=0, tiled=True),
            lax.all_gather(w_out, "shard", axis=0, tiled=True),
        )

    def gather_ffn():
        return (
            lax.all_gather(w_gate, "shard", axis=0, tiled=True),
            lax.all_gather(w_up, "shard", axis=0, tiled=True),
            lax.all_gather(w_down, "shard", axis=0, tiled=True),
        )

    owned_feature = None
    owned_hidden = None
    stored_list = []
    acc_attn_gain = jnp.zeros((width,), jnp.float32)
    acc_ffn_gain = jnp.zeros((width,), jnp.float32)
    acc_bias = jnp.zeros((local_heads, 2), jnp.float32)
    outputs_list = []
    grads_list = []
    for micro_index in range(micro):
        attn_full = gather_attn()
        ffn_full = gather_ffn()
        query_full, key_full, value_full, out_full = attn_full
        gate_full, up_full, down_full = ffn_full
        length_row = lengths[micro_index]
        valid_rows = (row_index[None, :] < length_row[:, None]).astype(jnp.float32)[..., None]
        inputs_wide = tokens[micro_index].astype(jnp.float32)
        inverse_attn = lax.rsqrt(
            jnp.mean(inputs_wide * inputs_wide, axis=-1, keepdims=True) + EPSILON
        )
        normed_attn = (inputs_wide * inverse_attn * attn_gain).astype(jnp.bfloat16)

        def project(weight):
            projected = jnp.einsum(
                "std,de->set", normed_attn, weight, preferred_element_type=jnp.float32
            )
            return projected.reshape(seq_count, heads, head_dim, local_len)

        cosine_now = cosine_tok[micro_index][:, None]
        sine_now = sine_tok[micro_index][:, None]
        queries = rotate_cols(project(query_full), cosine_now, sine_now, False).astype(jnp.bfloat16)
        keys_rot = rotate_cols(project(key_full), cosine_now, sine_now, False).astype(jnp.bfloat16)
        values_tok = project(value_full).astype(jnp.bfloat16)
        query_heads, key_heads, value_heads = (
            lax.all_to_all(queries, "seq", split_axis=1, concat_axis=3, tiled=True),
            lax.all_to_all(keys_rot, "seq", split_axis=1, concat_axis=3, tiled=True),
            lax.all_to_all(values_tok, "seq", split_axis=1, concat_axis=3, tiled=True),
        )
        mixed_heads, log_totals = attend_many(
            query_heads, key_heads, value_heads, variates_full[micro_index], length_row, bias_local
        )
        mixed_tok = lax.all_to_all(
            mixed_heads, "seq", split_axis=3, concat_axis=1, tiled=True
        ).reshape(seq_count, width, local_len)
        attn_out = jnp.einsum(
            "sdt,de->ste", mixed_tok, out_full, preferred_element_type=jnp.float32
        )
        residual = inputs_wide + attn_out
        inverse_ffn = lax.rsqrt(jnp.mean(residual * residual, axis=-1, keepdims=True) + EPSILON)
        normed_ffn = (residual * inverse_ffn * ffn_gain).astype(jnp.bfloat16)
        gate_act = jnp.einsum(
            "std,df->stf", normed_ffn, gate_full, preferred_element_type=jnp.float32
        )
        up_act = jnp.einsum("std,df->stf", normed_ffn, up_full, preferred_element_type=jnp.float32)
        sigmoid_gate = jax.nn.sigmoid(gate_act)
        silu_gate = gate_act * sigmoid_gate
        hidden = (silu_gate * up_act).astype(jnp.bfloat16)
        ffn_out = jnp.einsum("stf,fd->std", hidden, down_full, preferred_element_type=jnp.float32)
        outputs_list.append(((residual + ffn_out) * valid_rows).astype(jnp.bfloat16))
        attn_back = gather_attn()
        ffn_back = gather_ffn()
        query_back, key_back, value_back, out_back = attn_back
        gate_back, up_back, down_back = ffn_back
        masked_cot = cotangent[micro_index].astype(jnp.float32) * valid_rows
        grad_ffn = masked_cot.astype(jnp.bfloat16)
        grad_hidden = jnp.einsum(
            "std,fd->stf", grad_ffn, down_back, preferred_element_type=jnp.float32
        )
        grad_gate_act = (
            grad_hidden * up_act * (sigmoid_gate + gate_act * sigmoid_gate * (1.0 - sigmoid_gate))
        ).astype(jnp.bfloat16)
        grad_up_act = (grad_hidden * silu_gate).astype(jnp.bfloat16)
        grad_normed_ffn = jnp.einsum(
            "stf,df->std", grad_gate_act, gate_back, preferred_element_type=jnp.float32
        ) + jnp.einsum("stf,df->std", grad_up_act, up_back, preferred_element_type=jnp.float32)
        grad_res_norm, gain_term = norm_back(grad_normed_ffn, residual, inverse_ffn, ffn_gain)
        acc_ffn_gain = acc_ffn_gain + gain_term
        grad_residual = masked_cot + grad_res_norm
        grad_attn = grad_residual.astype(jnp.bfloat16)
        grad_mixed_tok = jnp.einsum(
            "ste,de->sdt", grad_attn, out_back, preferred_element_type=jnp.float32
        )
        grad_mixed_tok = grad_mixed_tok.astype(jnp.bfloat16).reshape(
            seq_count, heads, head_dim, local_len
        )
        grad_mixed_heads = lax.all_to_all(
            grad_mixed_tok, "seq", split_axis=1, concat_axis=3, tiled=True
        )
        grad_q_heads, grad_k_heads, grad_v_heads, grad_bias_seq = backward_many(
            query_heads,
            key_heads,
            value_heads,
            grad_mixed_heads,
            variates_full[micro_index],
            places_full[micro_index],
            length_row,
            log_totals,
            bias_local,
        )
        acc_bias = acc_bias + jnp.sum(grad_bias_seq, axis=0)
        grad_q_tok, grad_k_tok, grad_v_tok = (
            lax.all_to_all(grad_q_heads, "seq", split_axis=3, concat_axis=1, tiled=True),
            lax.all_to_all(grad_k_heads, "seq", split_axis=3, concat_axis=1, tiled=True),
            lax.all_to_all(grad_v_heads, "seq", split_axis=3, concat_axis=1, tiled=True),
        )
        grad_q_tok = grad_q_tok.reshape(seq_count, width, local_len)
        grad_k_tok = grad_k_tok.reshape(seq_count, width, local_len)
        grad_v_tok = grad_v_tok.reshape(seq_count, width, local_len)
        grad_normed_attn = (
            jnp.einsum("set,de->std", grad_q_tok, query_back, preferred_element_type=jnp.float32)
            + jnp.einsum("set,de->std", grad_k_tok, key_back, preferred_element_type=jnp.float32)
            + jnp.einsum("set,de->std", grad_v_tok, value_back, preferred_element_type=jnp.float32)
        )
        grad_in_norm, attn_gain_term = norm_back(
            grad_normed_attn, inputs_wide, inverse_attn, attn_gain
        )
        acc_attn_gain = acc_attn_gain + attn_gain_term
        grads_list.append((grad_residual + grad_in_norm).astype(jnp.bfloat16))
        stored = (
            normed_attn,
            mixed_tok,
            normed_ffn,
            grad_q_tok,
            grad_k_tok,
            grad_v_tok,
            grad_attn,
            grad_gate_act,
            grad_up_act,
            hidden,
            grad_ffn,
        )
        stored_list.append(stored)
    total = None
    for stored_item in stored_list:
        total = add_trees(total, feature_terms(stored_item))
    owned_feature = lax.psum_scatter(total, ("shard", "seq"), scatter_dimension=0, tiled=True)
    total = None
    for stored_item in stored_list:
        total = add_trees(total, hidden_terms(stored_item))
    owned_hidden = lax.psum_scatter(total, ("shard", "seq"), scatter_dimension=0, tiled=True)
    grad_query = owned_feature[:, 0:width]
    grad_key = owned_feature[:, width : 2 * width]
    grad_value = owned_feature[:, 2 * width : 3 * width]
    grad_out = owned_feature[:, 3 * width : 4 * width]
    grad_gate = owned_feature[:, 4 * width : 4 * width + ffn_width]
    grad_up = owned_feature[:, 4 * width + ffn_width : 4 * width + 2 * ffn_width]
    bias_full = lax.dynamic_update_slice(
        jnp.zeros((heads, 2), jnp.float32), acc_bias, (seq_index * local_heads, jnp.int32(0))
    )
    grad_attn_gain, grad_ffn_gain, grad_bias = lax.psum(
        (acc_attn_gain, acc_ffn_gain, bias_full), ("shard", "seq")
    )
    return (
        jnp.stack(outputs_list),
        jnp.stack(grads_list),
        grad_attn_gain,
        grad_query,
        grad_key,
        grad_value,
        grad_out,
        grad_bias,
        grad_ffn_gain,
        grad_gate,
        grad_up,
        owned_hidden,
    )


def solution(mesh):
    in_specs = (
        P(None, "shard", "seq", None),
        P(None, "shard", "seq", None),
        P(None, "shard"),
        P(None, "shard", "seq"),
        P(None, "shard", "seq"),
        P(),
        P("shard", None),
        P("shard", None),
        P("shard", None),
        P("shard", None),
        P(),
        P(),
        P("shard", None),
        P("shard", None),
        P("shard", None),
    )
    out_specs = (
        P(None, "shard", "seq", None),
        P(None, "shard", "seq", None),
        P(),
        P(("shard", "seq"), None),
        P(("shard", "seq"), None),
        P(("shard", "seq"), None),
        P(("shard", "seq"), None),
        P(),
        P(),
        P(("shard", "seq"), None),
        P(("shard", "seq"), None),
        P(("shard", "seq"), None),
    )
    return jax.shard_map(
        on_device, mesh=mesh, in_specs=in_specs, out_specs=out_specs, check_vma=False
    )
```

profile of v0, /device:TPU:0, one launch (start us, length us, event | category | flops | bytes accessed | tf_op | source)
XLA Modules:
  0.0 2773.2 jit_solution(375376373354726978)
XLA Ops:
  13.2 21.7 all-gather.10.cloned.1.call-done
  42.0 17.1 all-gather.8.cloned.1.call-done
  79.1 23.9 all-to-all-done.5
  144.4 17.9 all-to-all-done.1
  170.5 21.7 all-to-all-done.6
  196.5 43.6 %all_gather.20 = s32[2,1,4096]{2,1,0:T(1,128)S(1)} all-gather(s32[2,1,512]{2,1,0:T(1,128)S(1)} %copy-done.108), channel_id=1, replica_groups=mesh['shard'=4,'seq'=8] {'seq'}, dimensions={2}, use_global_device_ids=true | all-gather | bytes 36864 | tf_op jit(solution)/shard_map/all_gather | solution.py:237
  248.7 160.1 %while.61 = (s32[]{:T(128)}, bf16[8,1,2,64,512]{4,3,2,1,0:T(8,128)(2,1)S(1)}, f32[8,1,2,512]{3,2,1,0:T(2,128)S(1)}, bf16[8,1,2,64,512]{4,3,2,1,0:T(8,128)(2,1)},...) while((s32[]{:T(128)}, ...), condition=%wide.region_10.11_spmd.clone, body=%wide.region_7.10_spmd.clone.sunk | while | flops 1151405056 | bytes 61152456 | solution.py:78
  426.4 159.9 %while.60 = (s32[]{:T(128)}, bf16[8,1,2,64,512]{4,3,2,1,0:T(8,128)(2,1)S(1)}, f32[8,1,2,512]{3,2,1,0:T(2,128)S(1)}, bf16[8,1,2,64,512]{4,3,2,1,0:T(8,128)(2,1)},...) while((s32[]{:T(128)}, ...), condition=%wide.region_4.5_spmd.clone, body=%wide.region_1.4_spmd.clone.sunk | while | flops 1151405056 | bytes 61152456 | solution.py:78
  600.7 39.3 %all_gather.26 = s32[2,1,4096]{2,1,0:T(1,128)S(1)} all-gather(s32[2,1,512]{2,1,0:T(1,128)S(1)} %copy-done.96), channel_id=1, replica_groups=mesh['shard'=4,'seq'=8] {'seq'}, dimensions={2}, use_global_device_ids=true | all-gather | bytes 36864 | tf_op jit(solution)/shard_map/all_gather | solution.py:238
  667.6 10.4 fusion.182
  678.0 10.1 fusion.181
  688.2 16.1 multiply_convert_fusion.4
  713.2 10.2 multiply_reduce_fusion.3
  723.5 10.4 fusion.184
  733.9 10.1 fusion.183
  744.0 16.1 multiply_convert_fusion.2
  768.5 10.3 multiply_reduce_fusion.2
  816.8 429.6 %while.63 = (s32[]{:T(128)}, f32[1,2,64,4096]{3,2,1,0:T(8,128)S(1)}, f32[1,2,64,4096]{3,2,1,0:T(8,128)}, f32[1,2,2]{1,2,0:T(2,128)S(1)}, f32[8,1,2,64,512]{4,3,2...) while((s32[]{:T(128)}, ...), condition=%wide.region_24.25_spmd.clone, body=%wide.region_20.24_spmd.clone.sunk | while | flops 2752056320 | bytes 165464480 | solution.py:142
  820.0 9.0 fusion.319
  829.1 13.9 multiply_reduce_fusion.11
  843.0 13.8 convert_reduce_fusion.5
  882.7 13.9 multiply_reduce_fusion.11
  896.6 13.8 convert_reduce_fusion.5
  936.3 13.9 multiply_reduce_fusion.11
  950.3 13.8 convert_reduce_fusion.5
  989.9 13.9 multiply_reduce_fusion.11
  1003.9 13.8 convert_reduce_fusion.5
  1043.6 13.9 multiply_reduce_fusion.11
  1057.5 13.8 convert_reduce_fusion.5
  1097.2 13.9 multiply_reduce_fusion.11
  1111.1 13.8 convert_reduce_fusion.5
  1150.8 13.9 multiply_reduce_fusion.11
  1164.8 13.8 convert_reduce_fusion.5
  1204.5 13.9 multiply_reduce_fusion.11
  1218.4 13.8 convert_reduce_fusion.5
  1270.5 13.1 all-to-all-done.14
  1297.8 13.9 all-to-all-done.13
  1317.6 429.1 %while.62 = (s32[]{:T(128)}, f32[1,2,64,4096]{3,2,1,0:T(8,128)S(1)}, f32[1,2,64,4096]{3,2,1,0:T(8,128)}, f32[1,2,2]{1,2,0:T(2,128)S(1)}, f32[8,1,2,64,512]{4,3,2...) while((s32[]{:T(128)}, ...), condition=%wide.region_17.18_spmd.clone, body=%wide.region_13.17_spmd.clone.sunk | while | flops 2752056320 | bytes 165464480 | solution.py:142
  1329.4 13.9 multiply_reduce_fusion.10
  1343.3 13.8 convert_reduce_fusion.4
  1383.0 13.9 multiply_reduce_fusion.10
  1396.9 13.8 convert_reduce_fusion.4
  1436.6 13.9 multiply_reduce_fusion.10
  1450.5 13.8 convert_reduce_fusion.4
  1490.2 13.9 multiply_reduce_fusion.10
  1504.1 13.8 convert_reduce_fusion.4
  1543.8 13.9 multiply_reduce_fusion.10
  1557.7 13.8 convert_reduce_fusion.4
  1597.4 13.9 multiply_reduce_fusion.10
  1611.3 13.8 convert_reduce_fusion.4
  1651.0 13.9 multiply_reduce_fusion.10
  1664.9 13.8 convert_reduce_fusion.4
  1704.6 13.9 multiply_reduce_fusion.10
  1718.5 13.8 convert_reduce_fusion.4
  1770.5 15.7 all-to-all-done.10
  1796.2 19.5 all-to-all-done.9
  1924.3 49.2 %add.297 = f32[1024,12288]{1,0:T(8,128)} add(f32[1024,12288]{1,0:T(8,128)} %convolution_dynamic-update-slice_fusion.2, f32[1024,12288]{1,0:T(8,128)} %convolution_dynamic-update-slice_fusion) | non-fusion elementwise | flops 12582912 | bytes 150994944 | tf_op jit(solution)/shard_map/add | solution.py:208
  1974.2 16.9 fusion.154
  1991.0 17.4 convolution_add_fusion
  2009.1 12.7 fusion.138
  2021.8 9.5 fusion.139
  2048.2 44.2 %all-reduce = (f32[1024]{0:T(1024)}, f32[16,2]{0,1:T(2,128)}, f32[1024]{0:T(1024)}) all-reduce(f32[1024]{0:T(1024)S(1)} %add.296, f32[16,2]{0,1:T(2,128)S(1)} %dynamic_update_slice.24, f32[1024]{0:T(1024)S(1)} %add.300), channel_id=1, replica_groups=mesh['shard'=4,'seq'=8] {'shard','seq'}, use_global_device_ids=true, to_apply=%region_28.29 | all-reduce | flops 2080 | bytes 16640 | tf_op jit(solution)/shard_map/psum | solution.py:408
  2098.1 308.4 %reduce-scatter.3.cloned.1.call-done = f32[32,12288]{1,0:T(8,128)} async-done(((f32[1024,12288]{1,0:T(8,128)}), f32[32,12288]{1,0:T(8,128)}) %reduce-scatter.3.cloned.1.call-update) | async-done | bytes 1572880 | tf_op jit(solution)/shard_map/reduce_scatter | solution.py:394
  2410.6 355.8 %reduce-scatter.5.cloned.1.call-done = f32[128,1024]{1,0:T(8,128)} async-done(((f32[4096,1024]{1,0:T(8,128)}), f32[128,1024]{1,0:T(8,128)}) %reduce-scatter.5.cloned.1.call-update) | async-done | bytes 524304 | tf_op jit(solution)/shard_map/reduce_scatter | solution.py:398
  (807 shorter events, 1147.3 us)
Async XLA Ops:
  7.2 232.9 %copy-start = (f32[16,2]{0,1:T(2,128)S(1)}, f32[16,2]{0,1:T(2,128)}, u32[]{:S(2)}) copy-start(f32[16,2]{0,1:T(2,128)} %param.33) | copy-start | bytes 388
  7.2 27.7 all-gather.10.cloned.1.call-start
  7.9 51.2 %all-gather.8.cloned.1.call-start = ((), (), s32[]{:S(2)}) async-start(), calls=%async_computation.18 | async-start | bytes 2621440 | tf_op jit(solution)/shard_map/all_gather | solution.py:247
  8.7 127.8 %all-gather.12.cloned.1.call-start = ((), (), s32[]{:S(2)}) async-start(), calls=%async_computation.20 | async-start | bytes 2621440 | tf_op jit(solution)/shard_map/all_gather | solution.py:249
  9.4 651.4 %all-gather.14.cloned.1.call-start = ((), (), s32[]{:S(2)}) async-start(), calls=%async_computation.21 | async-start | bytes 2621440 | tf_op jit(solution)/shard_map/all_gather | solution.py:250
  10.0 657.5 %all-gather.18.cloned.1.call-start = ((), (), s32[]{:S(2)}) async-start(), calls=%async_computation.23 | async-start | bytes 10485760 | tf_op jit(solution)/shard_map/all_gather | solution.py:256
  10.6 24.3 copy-start.106
  10.6 667.4 %all-gather.16.cloned.1.call-start = ((), (), s32[]{:S(2)}) async-start(), calls=%async_computation.22 | async-start | bytes 10485760 | tf_op jit(solution)/shard_map/all_gather | solution.py:255
  12.6 127.8 %copy-start.98 = (f32[512]{0:T(512)}, f32[512]{0:T(512)S(1)}, u32[]{:S(2)}) copy-start(f32[512]{0:T(512)S(1)} %get-tuple-element.829) | copy-start | bytes 6148
  12.6 153.9 %copy-start.101 = (f32[512]{0:T(512)}, f32[512]{0:T(512)S(1)}, u32[]{:S(2)}) copy-start(f32[512]{0:T(512)S(1)} %get-tuple-element.845) | copy-start | bytes 6148
  71.3 31.7 %all-to-all-start.5 = ((bf16[1,16,64,512]{3,2,0,1:T(8,128)(2,1)}), bf16[1,16,64,512]{3,2,0,1:T(8,128)(2,1)S(1)}, u32[]{:S(2)}, u32[]{:S(2)}) async-start(bf16[1,16,64,512]{3,2,0,1:T(8,128)(2,1)} %maximum_bitcast_fusion.3), calls=%async_computation.5 | async-start | bytes 2097152 | tf_op jit(solution)/shard_map/all_to_all | solution.py:294
  103.0 29.9 %all-to-all-start.4 = ((bf16[1,16,64,512]{3,2,0,1:T(8,128)(2,1)}), bf16[1,16,64,512]{3,2,0,1:T(8,128)(2,1)}, u32[]{:S(2)}, u32[]{:S(2)}) async-start(bf16[1,16,64,512]{3,2,0,1:T(8,128)(2,1)} %maximum_bitcast_fusion.2), calls=%async_computation.4 | async-start | bytes 2097152 | tf_op jit(solution)/shard_map/all_to_all | solution.py:293
  132.9 29.4 %all-to-all-start.1 = ((bf16[1,16,64,512]{3,2,0,1:T(8,128)(2,1)}), bf16[1,16,64,512]{3,2,0,1:T(8,128)(2,1)S(1)}, u32[]{:S(2)}, u32[]{:S(2)}) async-start(bf16[1,16,64,512]{3,2,0,1:T(8,128)(2,1)} %maximum_bitcast_fusion.1), calls=%async_computation.1 | async-start | bytes 2097152 | tf_op jit(solution)/shard_map/all_to_all | solution.py:294
  162.3 29.9 %all-to-all-start.6 = ((bf16[1,16,64,512]{3,2,0,1:T(8,128)(2,1)}), bf16[1,16,64,512]{3,2,0,1:T(8,128)(2,1)}, u32[]{:S(2)}, u32[]{:S(2)}) async-start(bf16[1,16,64,512]{3,2,0,1:T(8,128)(2,1)} %fusion.135), calls=%async_computation.6 | async-start | bytes 2097152 | tf_op jit(solution)/shard_map/all_to_all | solution.py:295
  170.5 26.0 copy-start.108
  170.5 69.7 %copy-start.113 = (s32[2,1]{0,1:T(1,128)S(1)}, s32[2,1]{0,1:T(1,128)}, u32[]{:S(2)}) copy-start(s32[2,1]{0,1:T(1,128)} %param.25) | copy-start | bytes 28
  170.5 70.9 %copy-start.76 = (bf16[1,16,32,512]{3,2,1,0:T(8,128)(2,1)S(1)}, bf16[1,16,32,512]{3,2,1,0:T(8,128)(2,1)}, u32[]{:S(2)}) copy-start(bf16[1,16,32,512]{3,2,1,0:T(8,128)(2,1)} %get-tuple-element.807) | copy-start | bytes 1572868
  170.5 70.9 %copy-start.77 = (bf16[1,16,32,512]{3,2,1,0:T(8,128)(2,1)S(1)}, bf16[1,16,32,512]{3,2,1,0:T(8,128)(2,1)}, u32[]{:S(2)}) copy-start(bf16[1,16,32,512]{3,2,1,0:T(8,128)(2,1)} %get-tuple-element.808) | copy-start | bytes 1572868
  192.1 51.7 %all-to-all-start.2 = ((bf16[1,16,64,512]{3,2,0,1:T(8,128)(2,1)}), bf16[1,16,64,512]{3,2,0,1:T(8,128)(2,1)S(1)}, u32[]{:S(2)}, u32[]{:S(2)}) async-start(bf16[1,16,64,512]{3,2,0,1:T(8,128)(2,1)} %fusion.134), calls=%async_computation.2 | async-start | bytes 2097152 | tf_op jit(solution)/shard_map/all_to_all | solution.py:295
  195.7 46.7 %copy-start.54 = (bf16[1,16,64,512]{3,2,0,1:T(8,128)(2,1)S(1)}, bf16[1,16,64,512]{3,2,0,1:T(8,128)(2,1)}, u32[]{:S(2)}) copy-start(bf16[1,16,64,512]{3,2,0,1:T(8,128)(2,1)} %copy-done.53) | copy-start | bytes 3145732
  195.7 492.4 %all-gather.20.cloned.1.call-start = ((), (), s32[]{:S(2)}) async-start(), calls=%async_computation.24 | async-start | bytes 10485760 | tf_op jit(solution)/shard_map/all_gather | solution.py:257
  243.9 176.1 %all-to-all-start = ((bf16[1,16,64,512]{3,2,0,1:T(8,128)(2,1)}), bf16[1,16,64,512]{3,2,0,1:T(8,128)(2,1)}, u32[]{:S(2)}, u32[]{:S(2)}) async-start(bf16[1,16,64,512]{3,2,0,1:T(8,128)(2,1)} %maximum_bitcast_fusion), calls=%async_computation | async-start | bytes 2097152 | tf_op jit(solution)/shard_map/all_to_all | solution.py:293
  419.9 174.7 %all-to-all-start.7 = ((bf16[8,2,32768]{2,1,0:T(2,128)(2,1)}), bf16[8,2,32768]{2,1,0:T(2,128)(2,1)}, u32[]{:S(2)}, u32[]{:S(2)}) async-start(bf16[8,2,32768]{2,1,0:T(2,128)(2,1)} %reshape.1781), calls=%async_computation.7 | async-start | bytes 2097152 | tf_op jit(solution)/shard_map/all_to_all | solution.py:300
  594.7 57.6 %all-to-all-start.3 = ((bf16[8,2,32768]{2,1,0:T(2,128)(2,1)}), bf16[8,2,32768]{2,1,0:T(2,128)(2,1)S(1)}, u32[]{:S(2)}, u32[]{:S(2)}) async-start(bf16[8,2,32768]{2,1,0:T(2,128)(2,1)} %reshape.1783), calls=%async_computation.3 | async-start | bytes 2097152 | tf_op jit(solution)/shard_map/all_to_all | solution.py:300
  641.3 137.6 %copy-start.92 = (f32[512]{0:T(512)}, f32[512]{0:T(512)S(1)}, u32[]{:S(2)}) copy-start(f32[512]{0:T(512)S(1)} %get-tuple-element.850) | copy-start | bytes 6148
  641.3 137.6 %copy-start.104 = (f32[512]{0:T(512)}, f32[512]{0:T(512)S(1)}, u32[]{:S(2)}) copy-start(f32[512]{0:T(512)S(1)} %get-tuple-element.849) | copy-start | bytes 6148
  786.7 23.1 all-to-all-start.12
  810.8 444.9 %all-to-all-start.8 = ((bf16[1,16,64,512]{3,2,0,1:T(8,128)(2,1)}), bf16[1,16,64,512]{3,2,0,1:T(8,128)(2,1)}, u32[]{:S(2)}, u32[]{:S(2)}) async-start(bf16[1,16,64,512]{3,2,0,1:T(8,128)(2,1)} %bitcast.635), calls=%async_computation.8 | async-start | bytes 2097152 | tf_op jit(solution)/shard_map/all_to_all | solution.py:344
  843.0 13.8 copy-start.2
  896.6 13.8 copy-start.2
  950.3 13.8 copy-start.2
  1003.9 13.8 copy-start.2
  1057.5 13.8 copy-start.2
  1111.1 13.8 copy-start.2
  1164.8 13.8 copy-start.2
  1218.4 13.8 copy-start.2
  1255.6 27.9 %all-to-all-start.14 = ((bf16[8,2,32768]{2,1,0:T(2,128)(2,1)}), bf16[8,2,32768]{2,1,0:T(2,128)(2,1)S(1)}, u32[]{:S(2)}, u32[]{:S(2)}) async-start(bf16[8,2,32768]{2,1,0:T(2,128)(2,1)} %reshape.1787), calls=%async_computation.14 | async-start | bytes 2097152 | tf_op jit(solution)/shard_map/all_to_all | solution.py:361
  1283.6 28.2 %all-to-all-start.13 = ((bf16[8,2,32768]{2,1,0:T(2,128)(2,1)}), bf16[8,2,32768]{2,1,0:T(2,128)(2,1)}, u32[]{:S(2)}, u32[]{:S(2)}) async-start(bf16[8,2,32768]{2,1,0:T(2,128)(2,1)} %reshape.1785), calls=%async_computation.13 | async-start | bytes 2097152 | tf_op jit(solution)/shard_map/all_to_all | solution.py:360
  1297.8 19.7 copy-start.8
  1297.8 19.7 copy-start.64
  1311.7 444.1 %all-to-all-start.15 = ((bf16[8,2,32768]{2,1,0:T(2,128)(2,1)}), bf16[8,2,32768]{2,1,0:T(2,128)(2,1)}, u32[]{:S(2)}, u32[]{:S(2)}) async-start(bf16[8,2,32768]{2,1,0:T(2,128)(2,1)} %reshape.1789), calls=%async_computation.15 | async-start | bytes 2097152 | tf_op jit(solution)/shard_map/all_to_all | solution.py:362
  1343.3 13.8 copy-start.4
  1396.9 13.8 copy-start.4
  1450.5 13.8 copy-start.4
  1504.1 13.8 copy-start.4
  1557.7 13.8 copy-start.4
  1611.3 13.8 copy-start.4
  1664.9 13.8 copy-start.4
  1718.5 13.8 copy-start.4
  1755.9 30.4 %all-to-all-start.10 = ((bf16[8,2,32768]{2,1,0:T(2,128)(2,1)}), bf16[8,2,32768]{2,1,0:T(2,128)(2,1)S(1)}, u32[]{:S(2)}, u32[]{:S(2)}) async-start(bf16[8,2,32768]{2,1,0:T(2,128)(2,1)} %reshape.1793), calls=%async_computation.10 | async-start | bytes 2097152 | tf_op jit(solution)/shard_map/all_to_all | solution.py:361
  1766.0 24.5 copy-start.6
  1786.2 29.5 %all-to-all-start.9 = ((bf16[8,2,32768]{2,1,0:T(2,128)(2,1)}), bf16[8,2,32768]{2,1,0:T(2,128)(2,1)}, u32[]{:S(2)}, u32[]{:S(2)}) async-start(bf16[8,2,32768]{2,1,0:T(2,128)(2,1)} %reshape.1791), calls=%async_computation.9 | async-start | bytes 2097152 | tf_op jit(solution)/shard_map/all_to_all | solution.py:360
  1793.5 26.6 copy-start.46
  1815.8 37.5 %all-to-all-start.11 = ((bf16[8,2,32768]{2,1,0:T(2,128)(2,1)}), bf16[8,2,32768]{2,1,0:T(2,128)(2,1)}, u32[]{:S(2)}, u32[]{:S(2)}) async-start(bf16[8,2,32768]{2,1,0:T(2,128)(2,1)} %reshape.1795), calls=%async_computation.11 | async-start | bytes 2097152 | tf_op jit(solution)/shard_map/all_to_all | solution.py:362
  1820.0 586.5 %reduce-scatter.3.cloned.1.call-start = ((), (), s32[]{:S(2)}) async-start(), calls=%async_computation.25 | async-start | bytes 51904512 | tf_op jit(solution)/shard_map/reduce_scatter | solution.py:394
  1837.1 33.6 %copy-start.47 = (bf16[1,8,2,64,512]{4,3,2,1,0:T(8,128)(2,1)}, bf16[1,8,2,64,512]{4,3,2,1,0:T(8,128)(2,1)S(1)}, u32[]{:S(2)}) copy-start(bf16[1,8,2,64,512]{4,3,2,1,0:T(8,128)(2,1)S(1)} %copy.235) | copy-start | bytes 3145732
  1863.7 37.3 %copy-start.83 = (bf16[1,8,2,64,512]{4,3,2,1,0:T(8,128)(2,1)}, bf16[1,8,2,64,512]{4,3,2,1,0:T(8,128)(2,1)S(1)}, u32[]{:S(2)}) copy-start(bf16[1,8,2,64,512]{4,3,2,1,0:T(8,128)(2,1)S(1)} %copy.221) | copy-start | bytes 3145732
  1973.5 792.9 %reduce-scatter.5.cloned.1.call-start = ((), (), s32[]{:S(2)}) async-start(), calls=%async_computation.26 | async-start | bytes 17301504 | tf_op jit(solution)/shard_map/reduce_scatter | solution.py:398
  1974.2 16.9 copy-start.40
  1974.2 16.9 copy-start.44
  1974.2 16.9 copy-start.93
  2044.5 47.9 %copy-start.97 = (f32[512]{0:T(512)S(1)}, f32[512]{0:T(512)}, u32[]{:S(2)}) copy-start(f32[512]{0:T(512)} %get-tuple-element.828) | copy-start | bytes 6148
  2044.5 47.9 %copy-start.103 = (f32[512]{0:T(512)S(1)}, f32[512]{0:T(512)}, u32[]{:S(2)}) copy-start(f32[512]{0:T(512)} %get-tuple-element.846) | copy-start | bytes 6148
  2096.6 669.9 %copy-start.1 = (f32[16,2]{0,1:T(2,128)S(1)}, f32[16,2]{0,1:T(2,128)}, u32[]{:S(2)}) copy-start(f32[16,2]{0,1:T(2,128)} %param.33) | copy-start | bytes 388
  (119 other events, 503.2 us)
Sparse Core Ops, SparseCore 0:
  9.6 25.2 all-gather.9
  36.5 22.5 all-gather.7
  60.7 22.5 all-gather.11
  84.7 22.5 all-gather.13
  108.7 58.2 all-gather.17
  168.5 58.2 all-gather.15
  228.3 58.2 all-gather.19
  1973.6 432.8 reduce-scatter.2
  2409.4 357.0 reduce-scatter.4
where the time goes:
time: 2790 us; the launch traced here: 2770 us
  matrix products  1050 us (38%)
  waiting for transfers between devices  847 us (30%)
  other arithmetic  475 us (17%)
  local copies, waits for them, and re-layouts  177 us (6%)
  blocking collectives  127 us (5%)
  starting transfers between devices  75.5 us (3%)
    reduce_scatter x2, waiting for transfers between devices, on_device(): lax.psum_scatter(total, ('shard', 'seq'), scatter_dimension=0, tiled=True)  664 us
    dot_general x32, matrix products, block_scores(): jnp.einsum('hdq,hdk->hqk', query_block, keys_all, preferred_element_type=...  315 us
    reduce_sum x16, other arithmetic, one_block(): all_total = jnp.sum(grad_wide, axis=(1, 2))  221 us
    dot_general x16, matrix products, one_block(): jnp.einsum('hdq,hdk->hqk', grad_block, values_all, preferred_element_type...  145 us
    dot_general x16, matrix products, one_block(): jnp.einsum('hqk,hdq->hdk', probs_low, grad_block, preferred_element_type=...  123 us
    reduce_sum x16, other arithmetic, one_block(): total = jnp.sum(weights_exp, axis=-1, keepdims=True)  103 us
    dot_general x16, matrix products, one_block(): jnp.einsum('hqk,hdk->hdq', probs, values_all, preferred_element_type=jnp....  91.9 us
    unnamed x237, local copies, waits for them, and re-layouts  61.2 us
  transfers between devices with their start and end apart: 25, of which 13 were waited for; matrix products, arithmetic and copies ran while one was open for 53% of the time, Pallas kernels for 0%

commit v1 on v0

v1 whole, which is shorter than its diff:
```python
import functools
import math

import jax
import jax.numpy as jnp
from jax import lax
from jax.experimental import pallas as pl
from jax.experimental.pallas import tpu as pltpu
from jax.sharding import PartitionSpec as P

EPSILON = 1e-06
ROTARY_BASE = 10000.0
LOG2E = 1.4426950408889634
LN2 = 0.6931471805599453
CLASSES = 8
AUX = 16
EXTRA = 32
MASKED = -1.5e9
FAR = 1e30
F32 = jnp.float32
BF16 = jnp.bfloat16


def dot(a, b):
    return jnp.dot(a, b, preferred_element_type=F32)


def contract(a, b, da, db):
    return lax.dot_general(a, b, (((da,), (db,)), ((), ())), preferred_element_type=F32)


def pieces(x):
    high = x.astype(BF16).astype(F32)
    rest = x - high
    mid = rest.astype(BF16).astype(F32)
    low = (rest - mid).astype(BF16).astype(F32)
    return high, mid, low


def one_hot(row):
    classes = lax.broadcasted_iota(jnp.int32, (CLASSES, row.shape[1]), 0).astype(F32)
    return jnp.where(classes == row, 1.0, 0.0)


def rows_of(values, width):
    index = lax.broadcasted_iota(jnp.int32, (8, width), 0)
    out = jnp.zeros((8, width), F32)
    for at, value in enumerate(values):
        out = jnp.where(index == at, value, out)
    return out


def key_extra(row, start, length, other, same):
    width = row.shape[1]
    hot = one_hot(row)
    step = pieces(jnp.full((1, width), same - other, F32))
    base = pieces(jnp.full((1, width), other, F32))
    index = start + lax.broadcasted_iota(jnp.int32, (1, width), 1)
    mask = jnp.where(index < length, 0.0, MASKED)
    tail = rows_of(base + (mask, 1.0, 1.0, 1.0), width)
    return jnp.concatenate([hot * step[0], hot * step[1], hot * step[2], tail], axis=0).astype(BF16)


def query_extra(row, shift):
    hot = one_hot(row)
    tail = rows_of((1.0, 1.0, 1.0, 1.0) + shift, row.shape[1])
    return jnp.concatenate([hot, hot, hot, tail], axis=0).astype(BF16)


def forward_kernel(
    shape, len_ref, bias_ref, x_ref, *rest
):
    local, head_dim, block, aliased = shape
    if aliased:
        rest = rest[1:]
    mixed_ref, lse_ref, keys, vals, query, score, peak, total = rest
    count, _, width = x_ref.shape
    sub = block // width
    step = pl.program_id(0)
    length = len_ref[0]
    other = bias_ref[local, 0] * LOG2E
    same = bias_ref[local, 1] * LOG2E

    @pl.when(step == 0)
    def _():
        for b in range(count):
            at = pl.ds(b * width, width)
            row = x_ref[b, 3 * head_dim : 3 * head_dim + 1, :].astype(F32)
            extra = key_extra(row, b * width, length, other, same)
            full = jnp.concatenate([x_ref[b, head_dim : 2 * head_dim, :], extra], axis=0)
            keys[at, :] = full.T
            vals[0:head_dim, at] = x_ref[b, 2 * head_dim : 3 * head_dim, :]
        vals[head_dim:, :] = jnp.ones((16, vals.shape[1]), BF16)

    used = pl.cdiv(length, block)
    inside = step * block < length

    @pl.when(jnp.logical_not(inside))
    def _():
        mixed_ref[...] = jnp.zeros_like(mixed_ref)
        lse_ref[...] = jnp.full(lse_ref.shape, FAR, F32)

    @pl.when(inside)
    def _():
        for b in range(sub):
            at = slice(b * width, (b + 1) * width)
            row = x_ref[step * sub + b, 3 * head_dim : 3 * head_dim + 1, :].astype(F32)
            query[0:head_dim, at] = x_ref[step * sub + b, 0:head_dim, :]
            query[head_dim:, at] = query_extra(row, (0.0, 0.0, 0.0))
        peak[...] = jnp.full(peak.shape, -FAR, F32)
        total[...] = jnp.zeros_like(total)

        def span(j):
            return pl.ds(pl.multiple_of(j * block, block), block)

        def scores_of(j):
            return dot(keys[span(j), :], query[...])

        def one(j, now, ahead):
            if ahead:
                score[1 - now] = scores_of(j + 1)
            current = score[now]
            before = peak[...]
            top = jnp.maximum(before, jnp.max(current, axis=0, keepdims=True))
            weight = jnp.exp2(current - top).astype(BF16)
            peak[...] = top
            total[...] = total[...] * jnp.exp2(before - top) + dot(vals[:, span(j)], weight)

        score[0] = scores_of(0)
        pairs = (used - 1) // 2

        def pair(j, carry):
            one(2 * j, 0, True)
            one(2 * j + 1, 1, True)
            return carry

        lax.fori_loop(0, pairs, pair, 0)
        last = 2 * pairs

        @pl.when(used - last == 1)
        def _():
            one(last, 0, False)

        @pl.when(used - last == 2)
        def _():
            one(last, 0, True)
            one(last + 1, 1, False)

        mass = total[head_dim : head_dim + 1, :]
        mixed = (total[0:head_dim, :] / mass).astype(BF16)
        for b in range(sub):
            mixed_ref[b] = mixed[:, b * width : (b + 1) * width]
        lse_ref[0] = peak[...] + jnp.log2(mass)


def attend_forward(x, length, bias, mixed, local, heads_here, head_dim):
    count, rows, width = x.shape
    block = max(width, 512)
    seq_len = count * width
    blocks = seq_len // block
    depth = head_dim + EXTRA
    whole = pl.BlockSpec((count, rows, width), lambda i, *_: (0, 0, 0))
    operands = [length, bias, x]
    in_specs = [whole]
    aliases = {}
    if mixed is not None:
        operands.append(mixed)
        in_specs.append(pl.BlockSpec(memory_space=pl.ANY))
        aliases = {3: 0}
    return pl.pallas_call(
        functools.partial(forward_kernel, (local, head_dim, block, mixed is not None)),
        grid_spec=pltpu.PrefetchScalarGridSpec(
            num_scalar_prefetch=2,
            grid=(blocks,),
            in_specs=in_specs,
            out_specs=[
                pl.BlockSpec((block // width, head_dim, width), lambda i, *_: (i, local, 0)),
                pl.BlockSpec((1, 1, block), lambda i, *_: (i, 0, 0)),
            ],
            scratch_shapes=[
                pltpu.VMEM((seq_len, depth), BF16),
                pltpu.VMEM((head_dim + 16, seq_len), BF16),
                pltpu.VMEM((depth, block), BF16),
                pltpu.VMEM((2, block, block), F32),
                pltpu.VMEM((1, block), F32),
                pltpu.VMEM((head_dim + 16, block), F32),
            ],
        ),
        out_shape=[
            jax.ShapeDtypeStruct((count, heads_here * head_dim, width), BF16),
            jax.ShapeDtypeStruct((blocks, 1, block), F32),
        ],
        input_output_aliases=aliases,
        compiler_params=pltpu.CompilerParams(vmem_limit_bytes=40 << 20),
        cost_estimate=pl.CostEstimate(
            flops=8 * seq_len * seq_len * 256,
            bytes_accessed=x.size * 4,
            transcendentals=seq_len * seq_len,
        ),
        name="attend_forward",
    )(*operands)


def backward_kernel(
    shape, len_ref, bias_ref, x_ref, grad_ref, mixed_ref, lse_ref, out_ref, bias_out_ref,
    keys, keys_flat, vals, query, grads, query_rows, grad_rows, acc_keys, acc_vals, acc_query,
):
    local, head_dim, block = shape
    count, _, width = x_ref.shape
    sub = block // width
    step = pl.program_id(0)
    length = len_ref[0]
    other = bias_ref[local, 0] * LOG2E
    same = bias_ref[local, 1] * LOG2E

    @pl.when(step == 0)
    def _():
        ones = jnp.ones((16, width), BF16)
        for b in range(count):
            at = pl.ds(b * width, width)
            row = x_ref[b, 3 * head_dim : 3 * head_dim + 1, :].astype(F32)
            extra = key_extra(row, b * width, length, other, same)
            here = x_ref[b, head_dim : 2 * head_dim, :]
            keys[at, :] = jnp.concatenate([here, extra], axis=0).T
            keys_flat[:, at] = here
            vals[at, :] = jnp.concatenate([x_ref[b, 2 * head_dim : 3 * head_dim, :], ones], axis=0).T
        acc_keys[...] = jnp.zeros_like(acc_keys)
        acc_vals[...] = jnp.zeros_like(acc_vals)

    used = pl.cdiv(length, block)
    inside = step * block < length

    @pl.when(jnp.logical_not(inside))
    def _():
        for b in range(sub):
            out_ref[step * sub + b, 0:head_dim, :] = jnp.zeros((head_dim, width), BF16)

    @pl.when(inside)
    def _():
        for b in range(sub):
            at = slice(b * width, (b + 1) * width)
            here = step * sub + b
            row = x_ref[here, 3 * head_dim : 3 * head_dim + 1, :].astype(F32)
            shift = pieces(-lse_ref[step][:, at])
            grad = grad_ref[here]
            delta = jnp.sum(grad.astype(F32) * mixed_ref[here].astype(F32), axis=0, keepdims=True)
            query[0:head_dim, at] = x_ref[here, 0:head_dim, :]
            query[head_dim:, at] = query_extra(row, shift)
            grads[0:head_dim, at] = grad
            tail = rows_of(pieces(-delta), width)
            grads[head_dim:, at] = jnp.concatenate([tail, jnp.zeros_like(tail)], axis=0).astype(BF16)
        query_rows[...] = query[...].T
        grad_rows[...] = grads[...].T
        acc_query[...] = jnp.zeros_like(acc_query)

        def one(j):
            at = pl.ds(pl.multiple_of(j * block, block), block)
            probs = jnp.exp2(dot(keys[at, :], query[...]))
            grad_probs = dot(vals[at, :], grads[...])
            grad_scores = (probs * grad_probs).astype(BF16)
            acc_vals[at, :] += dot(probs.astype(BF16), grad_rows[...])
            acc_keys[at, :] += dot(grad_scores, query_rows[...])
            acc_query[...] += dot(keys_flat[:, at], grad_scores)

        def pair(j, carry):
            one(2 * j)
            one(2 * j + 1)
            return carry

        lax.fori_loop(0, used // 2, pair, 0)

        @pl.when(used % 2 == 1)
        def _():
            one(used - 1)

        grad_query = (acc_query[...] * (1.0 / math.sqrt(head_dim))).astype(BF16)
        for b in range(sub):
            out_ref[step * sub + b, 0:head_dim, :] = grad_query[:, b * width : (b + 1) * width]

    @pl.when(step == pl.num_programs(0) - 1)
    def _():
        same_total = jnp.zeros((CLASSES, width), F32)
        all_total = jnp.zeros((CLASSES, width), F32)
        for b in range(count):
            at = pl.ds(b * width, width)
            row = x_ref[b, 3 * head_dim : 3 * head_dim + 1, :].astype(F32)
            flat = acc_keys[at, :].T
            out_ref[b, head_dim : 2 * head_dim, :] = (flat[0:head_dim] * LN2).astype(BF16)
            out_ref[b, 2 * head_dim : 3 * head_dim, :] = acc_vals[at, :].T[0:head_dim].astype(BF16)
            by_class = flat[head_dim : head_dim + CLASSES]
            all_total += by_class
            same_total += by_class * one_hot(row)
        both = jnp.concatenate(
            [
                jnp.broadcast_to(jnp.sum(same_total, keepdims=True), (1, 128)),
                jnp.broadcast_to(jnp.sum(all_total, keepdims=True), (1, 128)),
                jnp.zeros((6, 128), F32),
            ],
            axis=0,
        )
        bias_out_ref[...] = both


def attend_backward(x, grad, mixed, lse, length, bias, local, head_dim):
    count, rows, width = x.shape
    blocks, _, block = lse.shape
    seq_len = count * width
    depth = head_dim + EXTRA

    def whole(a):
        return pl.BlockSpec(a.shape, lambda i, *_: (0,) * a.ndim)

    head_spec = pl.BlockSpec((count, head_dim, width), lambda i, *_: (0, local, 0))
    return pl.pallas_call(
        functools.partial(backward_kernel, (local, head_dim, block)),
        grid_spec=pltpu.PrefetchScalarGridSpec(
            num_scalar_prefetch=2,
            grid=(blocks,),
            in_specs=[whole(x), head_spec, head_spec, whole(lse)],
            out_specs=[
                pl.BlockSpec((count, 3 * head_dim, width), lambda i, *_: (0, 0, 0)),
                pl.BlockSpec((8, 128), lambda i, *_: (0, 0)),
            ],
            scratch_shapes=[
                pltpu.VMEM((seq_len, depth), BF16),
                pltpu.VMEM((head_dim, seq_len), BF16),
                pltpu.VMEM((seq_len, head_dim + 16), BF16),
                pltpu.VMEM((depth, block), BF16),
                pltpu.VMEM((head_dim + 16, block), BF16),
                pltpu.VMEM((block, depth), BF16),
                pltpu.VMEM((block, head_dim + 16), BF16),
                pltpu.VMEM((seq_len, depth), F32),
                pltpu.VMEM((seq_len, head_dim + 16), F32),
                pltpu.VMEM((head_dim, block), F32),
            ],
        ),
        out_shape=[
            jax.ShapeDtypeStruct((count, 3 * head_dim, width), BF16),
            jax.ShapeDtypeStruct((8, 128), F32),
        ],
        compiler_params=pltpu.CompilerParams(vmem_limit_bytes=48 << 20),
        cost_estimate=pl.CostEstimate(
            flops=20 * seq_len * seq_len * 256,
            bytes_accessed=x.size * 6,
            transcendentals=seq_len * seq_len,
        ),
        name="attend_backward",
    )(length, bias, x, grad, mixed, lse)


def rotary_tables(places, half_dim):
    frequency = jnp.exp(-math.log(ROTARY_BASE) * jnp.arange(half_dim, dtype=F32) / half_dim)
    angles = places.astype(F32)[None, :] * frequency[:, None]
    return jnp.cos(angles), jnp.sin(angles)


def rotate(values, cosine, sine, reverse):
    half_dim = values.shape[-2] // 2
    first = values[..., :half_dim, :]
    second = values[..., half_dim:, :]
    if reverse:
        parts = [first * cosine + second * sine, second * cosine - first * sine]
    else:
        parts = [first * cosine - second * sine, second * cosine + first * sine]
    return jnp.concatenate(parts, axis=-2)


def norm_back(grad_normed, inputs, inverse, gain):
    scaled = grad_normed * gain
    grad_inputs = inverse * scaled - inputs * (inverse * inverse * inverse) * jnp.mean(
        scaled * inputs, axis=-1, keepdims=True
    )
    return grad_inputs, jnp.sum(grad_normed * inputs * inverse, axis=0)


def on_device(
    tokens, cotangent, lengths, variates, positions, attn_gain, w_query, w_key, w_value, w_out,
    bias_table, ffn_gain, w_gate, w_up, w_down,
):
    micro, seqs, width, model = tokens.shape
    heads = bias_table.shape[0]
    head_dim = model // heads
    count = lax.axis_size("seq")
    here = heads // count
    ffn = w_gate.shape[1]
    seq_index = lax.axis_index("seq")
    bias_here = lax.dynamic_slice_in_dim(bias_table, seq_index * here, here, 0)
    row_index = seq_index * width + jnp.arange(width, dtype=jnp.int32)
    units = [(m, s) for m in range(micro) for s in range(seqs)]

    def gather(weight):
        return lax.all_gather(weight, "shard", axis=0, tiled=True)

    def exchange(values):
        return lax.all_to_all(values, "seq", split_axis=0, concat_axis=0, tiled=True)

    query_full, key_full, value_full = gather(w_query), gather(w_key), gather(w_value)
    out_full, gate_full, up_full, down_full = (
        gather(w_out), gather(w_gate), gather(w_up), gather(w_down)
    )

    first = []
    for m, s in units:
        inputs = tokens[m, s].astype(F32)
        inverse = lax.rsqrt(jnp.mean(inputs * inputs, axis=-1, keepdims=True) + EPSILON)
        normed = (inputs * inverse * attn_gain).astype(BF16)
        cosine, sine = rotary_tables(positions[m, s], head_dim // 2)

        def project(weight):
            return contract(weight, normed, 0, 1).reshape(heads, head_dim, width)

        scale = LOG2E / math.sqrt(head_dim)
        query = (rotate(project(query_full), cosine, sine, False) * scale).astype(BF16)
        key = rotate(project(key_full), cosine, sine, False).astype(BF16)
        value = project(value_full).astype(BF16)
        extra = jnp.broadcast_to(variates[m, s].astype(BF16)[None, None, :], (heads, AUX, width))
        packed = jnp.concatenate([query, key, value, extra], axis=1)
        packed = packed.reshape(count, here, 3 * head_dim + AUX, width)
        sent = [exchange(packed[:, h]) for h in range(here)]
        first.append((normed, inverse, cosine, sine, sent))

    attended = []
    for (m, s), item in zip(units, first):
        sent = item[4]
        length = lengths[m, s].reshape(1)
        mixed = None
        sums = []
        for h in range(here):
            mixed, lse = attend_forward(sent[h], length, bias_here, mixed, h, here, head_dim)
            sums.append(lse)
        mixed_tok = exchange(mixed).reshape(model, width)
        attended.append((mixed, sums, mixed_tok))

    outputs = [[None] * seqs for _ in range(micro)]
    middle = []
    acc_ffn_gain = jnp.zeros((model,), F32)
    for (m, s), (mixed, sums, mixed_tok) in zip(units, attended):
        valid = (row_index < lengths[m, s]).astype(F32)[:, None]
        inputs = tokens[m, s].astype(F32)
        residual = inputs + contract(mixed_tok, out_full, 0, 0)
        inverse = lax.rsqrt(jnp.mean(residual * residual, axis=-1, keepdims=True) + EPSILON)
        normed = (residual * inverse * ffn_gain).astype(BF16)
        gate = dot(normed, gate_full)
        up = dot(normed, up_full)
        sigmoid = jax.nn.sigmoid(gate)
        silu = gate * sigmoid
        hidden = (silu * up).astype(BF16)
        outputs[m][s] = ((residual + dot(hidden, down_full)) * valid).astype(BF16)
        masked = cotangent[m, s].astype(F32) * valid
        grad_ffn = masked.astype(BF16)
        grad_hidden = contract(grad_ffn, down_full, 1, 1)
        grad_gate = (grad_hidden * up * (sigmoid + silu * (1.0 - sigmoid))).astype(BF16)
        grad_up = (grad_hidden * silu).astype(BF16)
        grad_normed = contract(grad_gate, gate_full, 1, 1) + contract(grad_up, up_full, 1, 1)
        grad_res, gain_term = norm_back(grad_normed, residual, inverse, ffn_gain)
        acc_ffn_gain = acc_ffn_gain + gain_term
        grad_residual = masked + grad_res
        grad_attn = grad_residual.astype(BF16)
        grad_mixed = contract(out_full, grad_attn, 1, 1).astype(BF16)
        grad_heads = exchange(grad_mixed.reshape(count, here * head_dim, width))
        middle.append((normed, hidden, grad_ffn, grad_gate, grad_up, grad_residual, grad_attn, grad_heads))

    def joined(parts):
        return parts[0] if len(parts) == 1 else jnp.concatenate(parts, axis=0)

    normed_all = joined([item[0] for item in middle])
    hidden_all = joined([item[1] for item in middle])
    ffn_all = joined([item[2] for item in middle])
    devices = lax.axis_size("shard") * count
    rows = model // devices
    down_rows = ffn // devices
    fold = down_rows // rows

    def spread(total):
        split = total.reshape(devices, rows, fold, ffn // fold)
        return jnp.swapaxes(split, 1, 2).reshape(ffn, ffn // fold)

    gate_term = contract(normed_all, joined([item[3] for item in middle]), 0, 0).astype(BF16)
    up_term = contract(normed_all, joined([item[4] for item in middle]), 0, 0).astype(BF16)
    down_term = contract(hidden_all, ffn_all, 0, 0).astype(BF16)
    ffn_terms = jnp.concatenate([down_term, spread(gate_term), spread(up_term)], axis=1)
    ffn_owned = lax.psum_scatter(ffn_terms, ("shard", "seq"), scatter_dimension=0, tiled=True)

    grads = [[None] * seqs for _ in range(micro)]
    acc_attn_gain = jnp.zeros((model,), F32)
    acc_bias = jnp.zeros((here, 2), F32)
    returned = []
    for (m, s), before, (mixed, sums, _), item in zip(units, first, attended, middle):
        sent = before[4]
        length = lengths[m, s].reshape(1)
        back = []
        terms = []
        for h in range(here):
            packed, both = attend_backward(
                sent[h], item[7], mixed, sums[h], length, bias_here, h, head_dim
            )
            back.append(exchange(packed))
            terms.append(jnp.stack([both[1, 0] - both[0, 0], both[0, 0]]))
        acc_bias = acc_bias + jnp.stack(terms)
        returned.append(back)
    for (m, s), before, item, back in zip(units, first, middle, returned):
        normed, inverse, cosine, sine, _ = before
        grad_residual = item[5]
        full = jnp.stack(back, axis=1).reshape(heads, 3, head_dim, width)
        grad_q = rotate(full[:, 0].astype(F32), cosine, sine, True).astype(BF16).reshape(model, width)
        grad_k = rotate(full[:, 1].astype(F32), cosine, sine, True).astype(BF16).reshape(model, width)
        grad_v = full[:, 2].reshape(model, width)
        grad_normed = (
            contract(grad_q, query_full, 0, 1)
            + contract(grad_k, key_full, 0, 1)
            + contract(grad_v, value_full, 0, 1)
        )
        inputs = tokens[m, s].astype(F32)
        grad_in, gain_term = norm_back(grad_normed, inputs, inverse, attn_gain)
        acc_attn_gain = acc_attn_gain + gain_term
        grads[m][s] = (grad_residual + grad_in).astype(BF16)
        returned[m * seqs + s] = (grad_q, grad_k, grad_v)

    attn_normed = joined([item[0] for item in first])
    grad_cols = [jnp.concatenate([item[i] for item in returned], axis=1) for i in range(3)]
    terms = [contract(attn_normed, cols, 0, 1) for cols in grad_cols]
    mixed_cols = jnp.concatenate([item[2] for item in attended], axis=1)
    terms.append(contract(mixed_cols, joined([item[6] for item in middle]), 1, 0))
    pad = (-(4 * model)) % 384
    attn_terms = jnp.concatenate(terms + [jnp.zeros((model, pad), F32)], axis=1).astype(BF16)
    attn_owned = lax.psum_scatter(attn_terms, ("shard", "seq"), scatter_dimension=0, tiled=True)

    bias_full = lax.dynamic_update_slice(
        jnp.zeros((heads, 2), F32), acc_bias, (seq_index * here, jnp.int32(0))
    )
    grad_attn_gain, grad_ffn_gain, grad_bias = lax.psum(
        (acc_attn_gain, acc_ffn_gain, bias_full), ("shard", "seq")
    )

    def unspread(part):
        return jnp.swapaxes(part.reshape(fold, rows, ffn // fold), 0, 1).reshape(rows, ffn).astype(F32)

    part = ffn // fold
    attn_owned = attn_owned.astype(F32)
    return (
        jnp.stack([jnp.stack(item) for item in outputs]),
        jnp.stack([jnp.stack(item) for item in grads]),
        grad_attn_gain,
        attn_owned[:, 0:model],
        attn_owned[:, model : 2 * model],
        attn_owned[:, 2 * model : 3 * model],
        attn_owned[:, 3 * model : 4 * model],
        grad_bias,
        grad_ffn_gain,
        unspread(ffn_owned[:, model : model + part]),
        unspread(ffn_owned[:, model + part : model + 2 * part]),
        ffn_owned[:, 0:model].astype(F32),
    )


def solution(mesh):
    token_spec = P(None, "shard", "seq", None)
    row_spec = P("shard", None)
    in_specs = (
        token_spec, token_spec, P(None, "shard"), P(None, "shard", "seq"), P(None, "shard", "seq"),
        P(), row_spec, row_spec, row_spec, row_spec, P(), P(), row_spec, row_spec, row_spec,
    )
    owned = P(("shard", "seq"), None)
    out_specs = (
        token_spec, token_spec, P(), owned, owned, owned, owned, P(), P(), owned, owned, owned,
    )
    return jax.shard_map(
        on_device, mesh=mesh, in_specs=in_specs, out_specs=out_specs, check_vma=False
    )
```

time: 2790 us -> 1210 us (0.43)
  matrix products: 1050 us -> 245 us
  waiting for transfers between devices: 847 us -> 409 us
  other arithmetic: 475 us -> 56 us
  Pallas kernels: 0 us -> 145 us
    dot_general x154 -> x35, matrix products: 1050 us -> 245 us  [the longest x29 183 us: contract(): lax.dot_general(a, b, (((da,), (db,)), ((), ())), preferred_element_type=...]
    reduce_scatter x2 -> x1, waiting for transfers between devices: 664 us -> 147 us  [on_device(): lax.psum_scatter(ffn_terms, ('shard', 'seq'), scatter_dimension=0, tiled=...]
    reduce_sum x33 -> x1, other arithmetic: 324 us -> 0.48 us  [on_device(): jnp.mean(inputs * inputs, axis=-1, keepdims=True) + EPSILON]
    pallas_call x0 -> x8, Pallas kernels: none -> 145 us  [the longest x4 95.1 us: attend_backward(): pl.pallas_call(functools.partial(backward_kernel, (local, head_dim, block...]
    all_gather x2 -> x0, blocking collectives: 82.9 us -> none  [the longest x1 43.6 us: on_device(): lax.all_gather(variates, 'seq', axis=2, tiled=True)]
    all_to_all x16 -> x12, waiting for transfers between devices: 140 us -> 204 us  [exchange(): lax.all_to_all(values, 'seq', split_axis=0, concat_axis=0, tiled=True)]
    reshape x4 -> x6, local copies, waits for them, and re-layouts: 11.6 us -> 73.4 us  [the longest x4 50.5 us: spread(): split = total.reshape(devices, rows, fold, ffn // fold)]
    psum x1, blocking collectives: 44.2 us -> 101 us  [on_device(): lax.psum((acc_attn_gain, acc_ffn_gain, bias_full), ('shard', 'seq'))]
  transfers between devices with their start and end apart: 25 -> 21, of which waited for: 13 -> 16; matrix products, arithmetic and copies ran while one was open for 53% -> 26% of each run, Pallas kernels for 0% -> 12%
where the time goes in v1:
time: 1210 us
  waiting for transfers between devices  409 us (34%)
  matrix products  245 us (20%)
  local copies, waits for them, and re-layouts  173 us (14%)
  Pallas kernels  145 us (12%)
  blocking collectives  101 us (8%)
  other arithmetic  56 us (5%)
  starting transfers between devices  55 us (5%)
  between operations  20.5 us (2%)
    all_to_all x12, waiting for transfers between devices, exchange(): lax.all_to_all(values, 'seq', split_axis=0, concat_axis=0, tiled=True)  204 us
    dot_general x29, matrix products, contract(): lax.dot_general(a, b, (((da,), (db,)), ((), ())), preferred_element_type=...  183 us
    reduce_scatter x1, waiting for transfers between devices, on_device(): lax.psum_scatter(ffn_terms, ('shard', 'seq'), scatter_dimension=0, tiled=...  147 us
    psum x1, blocking collectives, on_device(): lax.psum((acc_attn_gain, acc_ffn_gain, bias_full), ('shard', 'seq'))  101 us
    pallas_call x4, Pallas kernels, attend_backward(): pl.pallas_call(functools.partial(backward_kernel, (local, head_dim, block...  95.1 us
    unnamed x184, local copies, waits for them, and re-layouts  70.3 us
    dot_general x6, matrix products, dot(): return jnp.dot(a, b, preferred_element_type=F32)  61.8 us
    all_to_all x12, starting transfers between devices, exchange(): lax.all_to_all(values, 'seq', split_axis=0, concat_axis=0, tiled=True)  54.3 us
  transfers between devices with their start and end apart: 21, of which 16 were waited for; matrix products, arithmetic and copies ran while one was open for 26% of the time, Pallas kernels for 12%

profile of v1, /device:TPU:0, one launch (start us, length us, event | category | flops | bytes accessed | tf_op | source)
XLA Modules:
  0.0 1205.1 jit_solution(12733035099974413406)
XLA Ops:
  15.9 19.0 %all-gather.10.cloned.1.call-done = bf16[1024,1024]{1,0:T(8,128)(2,1)} async-done(((bf16[256,1024]{1,0:T(8,128)(2,1)}), bf16[1024,1024]{1,0:T(8,128)(2,1)}) %all-gather.10.cloned.1.call-update) | async-done | bytes 2097168 | tf_op jit(solution)/shard_map/all_gather | solution.py:392
  41.0 18.1 %all-gather.8.cloned.1.call-done = bf16[1024,1024]{1,0:T(8,128)(2,1)} async-done(((bf16[256,1024]{1,0:T(8,128)(2,1)}), bf16[1024,1024]{1,0:T(8,128)(2,1)}) %all-gather.8.cloned.1.call-update) | async-done | bytes 2097168 | tf_op jit(solution)/shard_map/all_gather | solution.py:392
  66.2 17.1 %all-gather.12.cloned.1.call-done = bf16[1024,1024]{1,0:T(8,128)(2,1)} async-done(((bf16[256,1024]{1,0:T(8,128)(2,1)}), bf16[1024,1024]{1,0:T(8,128)(2,1)}) %all-gather.12.cloned.1.call-update) | async-done | bytes 2097168 | tf_op jit(solution)/shard_map/all_gather | solution.py:392
  93.4 5.8 all-to-all-start.4
  99.5 4.2 convolution_bitcast_fusion.2
  106.5 4.2 convolution_bitcast_fusion.3
  125.8 13.7 %all-to-all-done.4.x_ref = bf16[8,208,512]{2,1,0:T(8,128)(2,1)S(1)} async-done(((bf16[8,208,512]{2,1,0:T(8,128)(2,1)}), bf16[8,208,512]{2,1,0:T(8,128)(2,1)S(1)}, u32[]{:S(2)}, u32[]{:S(2)}) %all-to-all-start.4) | async-done | bytes 1703968 | tf_op jit(solution)/shard_map/all_to_all | solution.py:395
  143.1 8.1 attend_forward.6
  152.3 30.8 %all-to-all-done.1.x_ref = bf16[8,208,512]{2,1,0:T(8,128)(2,1)S(1)} async-done(((bf16[8,208,512]{2,1,0:T(8,128)(2,1)}), bf16[8,208,512]{2,1,0:T(8,128)(2,1)S(1)}, u32[]{:S(2)}, u32[]{:S(2)}) %all-to-all-start.1) | async-done | bytes 1703968 | tf_op jit(solution)/shard_map/all_to_all | solution.py:395
  183.1 4.3 all-to-all-start
  187.4 15.3 %attend_forward.4 = (bf16[8,128,512]{2,1,0:T(8,128)(2,1)S(1)}, f32[8,1,512]{2,1,0:T(1,128)S(1)}) custom-call(s32[1]{0:T(128)} %bitcast.1.len_ref, f32[2,2]{1,0:T(2,128)S(1)} %copy.163.bias_ref, bf16[8,208,512]{2,1,0:T(8,128)(2,1)S(1)} %all-to-all-done.1.x_ref), custom_call_target="tpu_custom_call" | custom-call | flops 34359738368 | bytes 3407872 | tf_op jit(solution)/shard_map/attend_forward/pallas_call | solution.py:170
  203.7 23.1 %all-to-all-done.x_ref = bf16[8,208,512]{2,1,0:T(8,128)(2,1)} async-done(((bf16[8,208,512]{2,1,0:T(8,128)(2,1)}), bf16[8,208,512]{2,1,0:T(8,128)(2,1)}, u32[]{:S(2)}, u32[]{:S(2)}) %all-to-all-start) | async-done | bytes 1703968 | tf_op jit(solution)/shard_map/all_to_all | solution.py:395
  226.8 4.3 all-to-all-start.3
  232.4 17.0 %attend_forward.5 = (bf16[8,128,512]{2,1,0:T(8,128)(2,1)S(1)}, f32[8,1,512]{2,1,0:T(1,128)S(1)}) custom-call(s32[1]{0:T(128)} %bitcast.1.len_ref, f32[2,2]{1,0:T(2,128)S(1)} %copy.163.bias_ref, bf16[8,208,512]{2,1,0:T(8,128)(2,1)} %all-to-all-done.x_ref, bf16[8,128,512]{2,1,0:T(8,128)(2,1)S(1)} %copy-done.10), custom_call_target="tpu_custom_call", output_to_operand_aliasing={{0}: (3, {})} | custom-call | flops 34359738368 | bytes 3407872 | tf_op jit(solution)/shard_map/attend_forward/pallas_call | solution.py:170
  250.4 20.2 %all-to-all-done.3.x_ref = bf16[8,208,512]{2,1,0:T(8,128)(2,1)} async-done(((bf16[8,208,512]{2,1,0:T(8,128)(2,1)}), bf16[8,208,512]{2,1,0:T(8,128)(2,1)}, u32[]{:S(2)}, u32[]{:S(2)}) %all-to-all-start.3) | async-done | bytes 1703968 | tf_op jit(solution)/shard_map/all_to_all | solution.py:395
  270.6 4.5 all-to-all-start.2
  276.3 9.6 attend_forward.7
  286.9 13.7 %all-to-all-done.2 = bf16[8,128,512]{2,1,0:T(8,128)(2,1)} async-done(((bf16[8,128,512]{2,1,0:T(8,128)(2,1)}), bf16[8,128,512]{2,1,0:T(8,128)(2,1)}, u32[]{:S(2)}, u32[]{:S(2)}) %all-to-all-start.2) | async-done | bytes 1048608 | tf_op jit(solution)/shard_map/all_to_all | solution.py:395
  300.7 4.2 all-to-all-start.5
  309.5 4.8 multiply_reduce_fusion.5
  314.3 16.1 %all-to-all-done.5 = bf16[8,128,512]{2,1,0:T(8,128)(2,1)} async-done(((bf16[8,128,512]{2,1,0:T(8,128)(2,1)}), bf16[8,128,512]{2,1,0:T(8,128)(2,1)}, u32[]{:S(2)}, u32[]{:S(2)}) %all-to-all-start.5) | async-done | bytes 1048608 | tf_op jit(solution)/shard_map/all_to_all | solution.py:395
  330.3 4.9 multiply_reduce_fusion.4
  336.6 11.6 fusion.119
  348.1 11.5 fusion.120
  359.6 16.4 %multiply_convert_fusion.2 = (bf16[512,4096]{1,0:T(8,128)(2,1)}, bf16[512,4096]{1,0:T(8,128)(2,1)}, bf16[512,4096]{1,0:T(8,128)(2,1)}) fusion(f32[512,4096]{1,0:T(8,128)} %fusion.119, f32[512,4096]{1,0:T(8,128)} %fusion.120, bf16[512,1024]{1,0:T(8,128)(2,1)} %get-tuple-element.151, bf16[4096,1024]{1,0:T(8,128)(2,1)} %all-gather.20.cloned.1.call-done), kind=kOutput, calls=%fused_computation.15 | convolution fusion | flops 4324327424 | bytes 38797312 | tf_op jit(solution)/shard_map/dot_general | solution.py:29
  376.0 8.4 fusion.123
  384.4 10.2 multiply_reduce_fusion.1
  394.7 10.5 fusion.121
  405.2 10.3 fusion.122
  415.5 16.0 %multiply_convert_fusion = (bf16[512,4096]{1,0:T(8,128)(2,1)}, bf16[512,4096]{1,0:T(8,128)(2,1)}, bf16[512,4096]{1,0:T(8,128)(2,1)}) fusion(f32[512,4096]{1,0:T(8,128)} %fusion.121, f32[512,4096]{1,0:T(8,128)} %fusion.122, bf16[512,1024]{1,0:T(8,128)(2,1)S(1)} %copy-done.32, bf16[4096,1024]{1,0:T(8,128)(2,1)} %all-gather.20.cloned.1.call-done), kind=kOutput, calls=%fused_computation.13 | convolution fusion | flops 4324327424 | bytes 38797312 | tf_op jit(solution)/shard_map/dot_general | solution.py:29
  431.5 8.4 fusion.126
  439.9 9.4 multiply_reduce_fusion
  458.1 4.5 all-to-all-start.9
  469.1 18.9 %all-to-all-done.9.grad_ref = bf16[8,128,512]{2,1,0:T(8,128)(2,1)} async-done(((bf16[8,128,512]{2,1,0:T(8,128)(2,1)}), bf16[8,128,512]{2,1,0:T(8,128)(2,1)}, u32[]{:S(2)}, u32[]{:S(2)}) %all-to-all-start.9) | async-done | bytes 1048608 | tf_op jit(solution)/shard_map/all_to_all | solution.py:395
  488.0 4.2 all-to-all-start.6
  493.4 16.4 %attend_backward.7 = (bf16[8,192,512]{2,1,0:T(8,128)(2,1)S(1)}, f32[8,128]{1,0:T(8,128)S(1)}) custom-call(s32[1]{0:T(128)} %bitcast.20.len_ref, f32[2,2]{1,0:T(2,128)S(1)} %copy.163.bias_ref, bf16[8,208,512]{2,1,0:T(8,128)(2,1)} %all-to-all-done.3.x_ref, bf16[8,128,512]{2,1,0:T(8,128)(2,1)} %all-to-all-done.9.grad_ref, bf16[8,128,512]{2,1,0:T(8,128)(2,1)S(1)} %copy-done.7, ...), custom_call_target="tpu_custom_call" | custom-call | flops 85899345920 | bytes 5111808 | tf_op jit(solution)/shard_map/attend_backward/pallas_call | solution.py:314
  511.0 6.6 all-to-all-done.6.grad_ref
  517.6 4.3 all-to-all-start.11
  523.1 15.9 %attend_backward.6 = (bf16[8,192,512]{2,1,0:T(8,128)(2,1)S(1)}, f32[8,128]{1,0:T(8,128)S(1)}) custom-call(s32[1]{0:T(128)} %bitcast.20.len_ref, f32[2,2]{1,0:T(2,128)S(1)} %copy.163.bias_ref, bf16[8,208,512]{2,1,0:T(8,128)(2,1)S(1)} %all-to-all-done.4.x_ref, bf16[8,128,512]{2,1,0:T(8,128)(2,1)} %all-to-all-done.9.grad_ref, ...), custom_call_target="tpu_custom_call" | custom-call | flops 85899345920 | bytes 5111808 | tf_op jit(solution)/shard_map/attend_backward/pallas_call | solution.py:314
  540.2 16.6 %all-to-all-done.11 = bf16[8,192,512]{2,1,0:T(8,128)(2,1)} async-done(((bf16[8,192,512]{2,1,0:T(8,128)(2,1)}), bf16[8,192,512]{2,1,0:T(8,128)(2,1)}, u32[]{:S(2)}, u32[]{:S(2)}) %all-to-all-start.11) | async-done | bytes 1572896 | tf_op jit(solution)/shard_map/all_to_all | solution.py:395
  556.9 5.2 all-to-all-start.10
  562.1 31.6 %attend_backward.5 = (bf16[8,192,512]{2,1,0:T(8,128)(2,1)}, f32[8,128]{1,0:T(8,128)S(1)}) custom-call(s32[1]{0:T(128)} %bitcast.1.len_ref, f32[2,2]{1,0:T(2,128)S(1)} %copy.163.bias_ref, bf16[8,208,512]{2,1,0:T(8,128)(2,1)} %all-to-all-done.x_ref, bf16[8,128,512]{2,1,0:T(8,128)(2,1)} %all-to-all-done.6.grad_ref, bf16[8,128,512]{2,1,0:T(8,128)(2,1)S(1)} %copy-done.12, ...), custom_call_target="tpu_custom_call" | custom-call | flops 85899345920 | bytes 5111808 | tf_op jit(solution)/shard_map/attend_backward/pallas_call | solution.py:314
  593.7 4.2 all-to-all-done.10
  598.0 5.7 all-to-all-start.8
  603.7 31.1 %attend_backward.4 = (bf16[8,192,512]{2,1,0:T(8,128)(2,1)}, f32[8,128]{1,0:T(8,128)S(1)}) custom-call(s32[1]{0:T(128)} %bitcast.1.len_ref, f32[2,2]{1,0:T(2,128)S(1)} %copy.163.bias_ref, bf16[8,208,512]{2,1,0:T(8,128)(2,1)S(1)} %all-to-all-done.1.x_ref, bf16[8,128,512]{2,1,0:T(8,128)(2,1)} %all-to-all-done.6.grad_ref, bf16[8,128,512]{2,1,0:T(8,128)(2,1)S(1)} %copy-done.12, ...), custom_call_target="tpu_custom_call" | custom-call | flops 85899345920 | bytes 5111808 | tf_op jit(solution)/shard_map/attend_backward/pallas_call | solution.py:314
  634.8 7.5 all-to-all-done.8
  651.2 32.2 %all-to-all-done.7 = bf16[8,192,512]{2,1,0:T(8,128)(2,1)S(1)} async-done(((bf16[8,192,512]{2,1,0:T(8,128)(2,1)}), bf16[8,192,512]{2,1,0:T(8,128)(2,1)S(1)}, u32[]{:S(2)}, u32[]{:S(2)}) %all-to-all-start.7) | async-done | bytes 1572896 | tf_op jit(solution)/shard_map/all_to_all | solution.py:395
  703.8 5.3 convert_dynamic-update-slice_fusion
  709.8 11.4 copy.159
  722.8 14.7 %fusion.12 = bf16[1024,4096]{1,0:T(8,128)(2,1)} fusion(bf16[512,4096]{1,0:T(8,128)(2,1)} %get-tuple-element.116, bf16[512,4096]{1,0:T(8,128)(2,1)} %get-tuple-element.113, bf16[512,1024]{1,0:T(8,128)(2,1)S(1)} %copy-done.81, bf16[512,1024]{1,0:T(8,128)(2,1)S(1)} %copy-done.34), kind=kOutput, calls=%fused_computation.21 | convolution fusion | flops 8615100416 | bytes 18874368 | tf_op jit(solution)/shard_map/dot_general | solution.py:29
  737.5 14.6 %reshape.365 = bf16[32,32,4,1024]{3,2,1,0:T(4,128)(2,1)} reshape(bf16[1024,4096]{1,0:T(8,128)(2,1)} %fusion.12) | data formatting | bytes 16777216 | tf_op jit(solution)/shard_map/reshape | solution.py:475
  752.1 10.4 copy.145
  762.5 11.3 copy.147
  773.8 14.9 %fusion.15 = bf16[1024,4096]{1,0:T(8,128)(2,1)} fusion(bf16[512,4096]{1,0:T(8,128)(2,1)} %get-tuple-element.117, bf16[512,4096]{1,0:T(8,128)(2,1)} %get-tuple-element.114, bf16[512,1024]{1,0:T(8,128)(2,1)S(1)} %copy-done.81, bf16[512,1024]{1,0:T(8,128)(2,1)S(1)} %copy-done.34), kind=kOutput, calls=%fused_computation.22 | convolution fusion | flops 8615100416 | bytes 18874368 | tf_op jit(solution)/shard_map/dot_general | solution.py:29
  788.7 14.8 %reshape.363 = bf16[32,32,4,1024]{3,2,1,0:T(4,128)(2,1)} reshape(bf16[1024,4096]{1,0:T(8,128)(2,1)} %fusion.15) | data formatting | bytes 16777216 | tf_op jit(solution)/shard_map/reshape | solution.py:475
  803.5 10.7 copy.144
  814.2 11.7 copy.146
  825.9 16.0 %fusion.18 = bf16[4096,1024]{0,1:T(8,128)(2,1)} fusion(bf16[512,4096]{1,0:T(8,128)(2,1)} %get-tuple-element.118, bf16[512,4096]{1,0:T(8,128)(2,1)} %get-tuple-element.115, bf16[512,1024]{1,0:T(8,128)(2,1)S(1)} %copy-done.33, bf16[512,1024]{1,0:T(8,128)(2,1)S(1)} %copy-done.31), kind=kOutput, calls=%fused_computation.23 | convolution fusion | flops 8615100416 | bytes 18874368 | tf_op jit(solution)/shard_map/dot_general | solution.py:29
  841.9 18.1 %pad_maximum_fusion = bf16[4096,3072]{0,1:T(8,128)(2,1)} fusion(bf16[4096,1024]{0,1:T(8,128)(2,1)} %copy.147, bf16[4096,1024]{0,1:T(8,128)(2,1)} %copy.146, bf16[4096,1024]{0,1:T(8,128)(2,1)} %fusion.18), kind=kLoop, calls=%fused_computation | loop fusion | flops 75497472 | bytes 50331648 | tf_op jit(solution)/shard_map/concatenate | solution.py:481
  860.0 30.8 %copy.161 = bf16[4096,3072]{1,0:T(8,128)(2,1)} copy(bf16[4096,3072]{0,1:T(8,128)(2,1)} %pad_maximum_fusion) | data formatting | bytes 50331648
  891.6 10.0 fusion.86
  901.6 7.9 fusion.85
  935.6 101.0 %all-reduce = (f32[1024]{0:T(1024)}, f32[16,2]{0,1:T(2,128)}, f32[1024]{0:T(1024)}) all-reduce(f32[1024]{0:T(1024)S(1)} %add.191, f32[16,2]{0,1:T(2,128)S(1)} %dynamic_update_slice.3, f32[1024]{0:T(1024)S(1)} %add.193), channel_id=1, replica_groups=mesh['shard'=4,'seq'=8] {'shard','seq'}, use_global_device_ids=true, to_apply=%region_10.0 | all-reduce | flops 2080 | bytes 16640 | tf_op jit(solution)/shard_map/psum | solution.py:531
  1047.3 147.0 %reduce-scatter.9.cloned.1.call-done = bf16[128,3072]{1,0:T(8,128)(2,1)} async-done(((bf16[4096,3072]{1,0:T(8,128)(2,1)}), bf16[128,3072]{1,0:T(8,128)(2,1)}) %reduce-scatter.9.cloned.1.call-update) | async-done | bytes 786448 | tf_op jit(solution)/shard_map/reduce_scatter | solution.py:482
  (295 shorter events, 153.0 us)
Async XLA Ops:
  7.2 92.1 %copy-start = (f32[16,2]{0,1:T(2,128)S(1)}, f32[16,2]{0,1:T(2,128)}, u32[]{:S(2)}) copy-start(f32[16,2]{0,1:T(2,128)} %param.25) | copy-start | bytes 388
  7.2 27.7 %all-gather.10.cloned.1.call-start = ((), (), s32[]{:S(2)}) async-start(), calls=%async_computation.15 | async-start | bytes 2621440 | tf_op jit(solution)/shard_map/all_gather | solution.py:392
  7.9 51.2 %all-gather.8.cloned.1.call-start = ((), (), s32[]{:S(2)}) async-start(), calls=%async_computation.14 | async-start | bytes 2621440 | tf_op jit(solution)/shard_map/all_gather | solution.py:392
  8.7 74.6 %all-gather.12.cloned.1.call-start = ((), (), s32[]{:S(2)}) async-start(), calls=%async_computation.16 | async-start | bytes 2621440 | tf_op jit(solution)/shard_map/all_gather | solution.py:392
  9.4 300.1 %all-gather.14.cloned.1.call-start = ((), (), s32[]{:S(2)}) async-start(), calls=%async_computation.17 | async-start | bytes 2621440 | tf_op jit(solution)/shard_map/all_gather | solution.py:392
  10.0 326.6 %all-gather.16.cloned.1.call-start = ((), (), s32[]{:S(2)}) async-start(), calls=%async_computation.18 | async-start | bytes 10485760 | tf_op jit(solution)/shard_map/all_gather | solution.py:392
  10.6 337.5 %all-gather.18.cloned.1.call-start = ((), (), s32[]{:S(2)}) async-start(), calls=%async_computation.19 | async-start | bytes 10485760 | tf_op jit(solution)/shard_map/all_gather | solution.py:392
  11.2 348.4 %all-gather.20.cloned.1.call-start = ((), (), s32[]{:S(2)}) async-start(), calls=%async_computation.20 | async-start | bytes 10485760 | tf_op jit(solution)/shard_map/all_gather | solution.py:392
  15.3 68.0 %copy-start.45 = (bf16[512,1024]{1,0:T(8,128)(2,1)}, bf16[512,1024]{1,0:T(8,128)(2,1)S(1)}, u32[]{:S(2)}) copy-start(bf16[512,1024]{1,0:T(8,128)(2,1)S(1)} %get-tuple-element.150) | copy-start | bytes 3145732
  15.8 72.8 %copy-start.56 = (f32[32,512]{1,0:T(8,128)}, f32[32,512]{1,0:T(8,128)S(1)}, u32[]{:S(2)}) copy-start(f32[32,512]{1,0:T(8,128)S(1)} %get-tuple-element.191) | copy-start | bytes 196612
  15.8 72.8 %copy-start.58 = (f32[32,512]{1,0:T(8,128)}, f32[32,512]{1,0:T(8,128)S(1)}, u32[]{:S(2)}) copy-start(f32[32,512]{1,0:T(8,128)S(1)} %get-tuple-element.192) | copy-start | bytes 196612
  15.9 102.6 %copy-start.52 = (f32[32,512]{1,0:T(8,128)}, f32[32,512]{1,0:T(8,128)S(1)}, u32[]{:S(2)}) copy-start(f32[32,512]{1,0:T(8,128)S(1)} %get-tuple-element.179) | copy-start | bytes 196612
  15.9 102.6 %copy-start.54 = (f32[32,512]{1,0:T(8,128)}, f32[32,512]{1,0:T(8,128)S(1)}, u32[]{:S(2)}) copy-start(f32[32,512]{1,0:T(8,128)S(1)} %get-tuple-element.180) | copy-start | bytes 196612
  93.4 6.0 copy-start.43
  93.4 46.0 %all-to-all-start.4 = ((bf16[8,208,512]{2,1,0:T(8,128)(2,1)}), bf16[8,208,512]{2,1,0:T(8,128)(2,1)S(1)}, u32[]{:S(2)}, u32[]{:S(2)}) async-start(bf16[8,208,512]{2,1,0:T(8,128)(2,1)} %get-tuple-element.121), calls=%async_computation.4 | async-start | bytes 3407872 | tf_op jit(solution)/shard_map/all_to_all | solution.py:395
  139.5 43.6 %all-to-all-start.1 = ((bf16[8,208,512]{2,1,0:T(8,128)(2,1)}), bf16[8,208,512]{2,1,0:T(8,128)(2,1)S(1)}, u32[]{:S(2)}, u32[]{:S(2)}) async-start(bf16[8,208,512]{2,1,0:T(8,128)(2,1)} %get-tuple-element.119), calls=%async_computation.1 | async-start | bytes 3407872 | tf_op jit(solution)/shard_map/all_to_all | solution.py:395
  183.1 43.7 %all-to-all-start = ((bf16[8,208,512]{2,1,0:T(8,128)(2,1)}), bf16[8,208,512]{2,1,0:T(8,128)(2,1)}, u32[]{:S(2)}, u32[]{:S(2)}) async-start(bf16[8,208,512]{2,1,0:T(8,128)(2,1)} %get-tuple-element.120), calls=%async_computation | async-start | bytes 3407872 | tf_op jit(solution)/shard_map/all_to_all | solution.py:395
  226.8 43.7 %all-to-all-start.3 = ((bf16[8,208,512]{2,1,0:T(8,128)(2,1)}), bf16[8,208,512]{2,1,0:T(8,128)(2,1)}, u32[]{:S(2)}, u32[]{:S(2)}) async-start(bf16[8,208,512]{2,1,0:T(8,128)(2,1)} %get-tuple-element.122), calls=%async_computation.3 | async-start | bytes 3407872 | tf_op jit(solution)/shard_map/all_to_all | solution.py:395
  270.6 30.1 %all-to-all-start.2 = ((bf16[8,128,512]{2,1,0:T(8,128)(2,1)}), bf16[8,128,512]{2,1,0:T(8,128)(2,1)}, u32[]{:S(2)}, u32[]{:S(2)}) async-start(bf16[8,128,512]{2,1,0:T(8,128)(2,1)} %copy-done.11), calls=%async_computation.2 | async-start | bytes 2097152 | tf_op jit(solution)/shard_map/all_to_all | solution.py:395
  300.7 29.7 %all-to-all-start.5 = ((bf16[8,128,512]{2,1,0:T(8,128)(2,1)}), bf16[8,128,512]{2,1,0:T(8,128)(2,1)}, u32[]{:S(2)}, u32[]{:S(2)}) async-start(bf16[8,128,512]{2,1,0:T(8,128)(2,1)} %copy-done.6), calls=%async_computation.5 | async-start | bytes 2097152 | tf_op jit(solution)/shard_map/all_to_all | solution.py:395
  305.6 143.8 %copy-start.64 = (f32[512]{0:T(512)}, f32[512]{0:T(512)S(1)}, u32[]{:S(2)}) copy-start(f32[512]{0:T(512)S(1)} %fusion.97) | copy-start | bytes 6148
  306.2 143.1 %copy-start.66 = (f32[512]{0:T(512)}, f32[512]{0:T(512)S(1)}, u32[]{:S(2)}) copy-start(f32[512]{0:T(512)S(1)} %fusion.98) | copy-start | bytes 6148
  330.3 4.9 copy-start.15
  330.3 4.9 copy-start.70
  376.0 8.4 copy-start.16
  376.0 8.4 copy-start.24
  376.0 8.4 copy-start.82
  394.7 10.5 copy-start.80
  405.2 10.3 copy-start.32
  431.5 8.4 copy-start.25
  439.9 9.4 copy-start.17
  439.9 9.4 copy-start.23
  439.9 9.4 copy-start.30
  449.4 4.2 copy-start.19
  458.1 29.8 %all-to-all-start.9 = ((bf16[8,128,512]{2,1,0:T(8,128)(2,1)}), bf16[8,128,512]{2,1,0:T(8,128)(2,1)}, u32[]{:S(2)}, u32[]{:S(2)}) async-start(bf16[8,128,512]{2,1,0:T(8,128)(2,1)} %bitcast.230), calls=%async_computation.9 | async-start | bytes 2097152 | tf_op jit(solution)/shard_map/all_to_all | solution.py:395
  488.0 29.7 %all-to-all-start.6 = ((bf16[8,128,512]{2,1,0:T(8,128)(2,1)}), bf16[8,128,512]{2,1,0:T(8,128)(2,1)}, u32[]{:S(2)}, u32[]{:S(2)}) async-start(bf16[8,128,512]{2,1,0:T(8,128)(2,1)} %bitcast.229), calls=%async_computation.6 | async-start | bytes 2097152 | tf_op jit(solution)/shard_map/all_to_all | solution.py:395
  517.6 39.2 %all-to-all-start.11 = ((bf16[8,192,512]{2,1,0:T(8,128)(2,1)}), bf16[8,192,512]{2,1,0:T(8,128)(2,1)}, u32[]{:S(2)}, u32[]{:S(2)}) async-start(bf16[8,192,512]{2,1,0:T(8,128)(2,1)} %copy-done.2), calls=%async_computation.11 | async-start | bytes 3145728 | tf_op jit(solution)/shard_map/all_to_all | solution.py:395
  540.2 21.9 %copy-start.12 = (bf16[8,128,512]{2,1,0:T(8,128)(2,1)S(1)}, bf16[8,128,512]{2,1,0:T(8,128)(2,1)}, u32[]{:S(2)}) copy-start(bf16[8,128,512]{2,1,0:T(8,128)(2,1)} %copy-done.11) | copy-start | bytes 3145732
  556.9 41.1 %all-to-all-start.10 = ((bf16[8,192,512]{2,1,0:T(8,128)(2,1)}), bf16[8,192,512]{2,1,0:T(8,128)(2,1)}, u32[]{:S(2)}, u32[]{:S(2)}) async-start(bf16[8,192,512]{2,1,0:T(8,128)(2,1)} %copy-done.3), calls=%async_computation.10 | async-start | bytes 3145728 | tf_op jit(solution)/shard_map/all_to_all | solution.py:395
  598.0 44.3 %all-to-all-start.8 = ((bf16[8,192,512]{2,1,0:T(8,128)(2,1)}), bf16[8,192,512]{2,1,0:T(8,128)(2,1)}, u32[]{:S(2)}, u32[]{:S(2)}) async-start(bf16[8,192,512]{2,1,0:T(8,128)(2,1)} %get-tuple-element.35), calls=%async_computation.8 | async-start | bytes 3145728 | tf_op jit(solution)/shard_map/all_to_all | solution.py:395
  642.3 41.1 %all-to-all-start.7 = ((bf16[8,192,512]{2,1,0:T(8,128)(2,1)}), bf16[8,192,512]{2,1,0:T(8,128)(2,1)S(1)}, u32[]{:S(2)}, u32[]{:S(2)}) async-start(bf16[8,192,512]{2,1,0:T(8,128)(2,1)} %get-tuple-element.33), calls=%async_computation.7 | async-start | bytes 3145728 | tf_op jit(solution)/shard_map/all_to_all | solution.py:395
  645.9 396.4 %reduce-scatter.7.cloned.1.call-start = ((), (), s32[]{:S(2)}) async-start(), calls=%async_computation.21 | async-start | bytes 8921088
  651.2 48.8 %copy-start.27 = (bf16[16,1,64,512]{3,2,1,0:T(8,128)(2,1)}, bf16[16,1,64,512]{3,2,1,0:T(8,128)(2,1)S(1)}, u32[]{:S(2)}) copy-start(bf16[16,1,64,512]{3,2,1,0:T(8,128)(2,1)S(1)} %get-tuple-element.126) | copy-start | bytes 3145732
  685.4 2.6 copy-start.21
  685.4 2.6 copy-start.57
  685.9 14.1 %copy-start.47 = (bf16[16,1,64,512]{3,2,1,0:T(8,128)(2,1)}, bf16[16,1,64,512]{3,2,1,0:T(8,128)(2,1)S(1)}, u32[]{:S(2)}) copy-start(bf16[16,1,64,512]{3,2,1,0:T(8,128)(2,1)S(1)} %get-tuple-element.123) | copy-start | bytes 3145732
  689.0 7.4 copy-start.37
  690.5 5.9 copy-start.39
  690.6 5.8 copy-start.41
  700.0 3.7 copy-start.49
  700.0 3.7 copy-start.51
  721.3 473.0 %reduce-scatter.9.cloned.1.call-start = ((), (), s32[]{:S(2)}) async-start(), calls=%async_computation.22 | async-start | bytes 25952256 | tf_op jit(solution)/shard_map/reduce_scatter | solution.py:482
  814.2 11.7 copy-start.31
  814.2 11.7 copy-start.33
  891.5 10.0 copy-start.18
  891.5 10.0 copy-start.65
  891.5 10.0 copy-start.83
  909.6 12.1 %copy-start.36 = (bf16[16,64,512]{2,1,0:T(8,128)(2,1)S(1)}, bf16[16,64,512]{2,1,0:T(8,128)(2,1)}, u32[]{:S(2)}) copy-start(bf16[16,64,512]{2,1,0:T(8,128)(2,1)} %copy-done.35) | copy-start | bytes 3145732
  921.6 3.1 copy-start.38
  921.6 3.1 copy-start.78
  931.8 3.8 copy-start.22
  931.8 104.8 %copy-start.71 = (f32[512]{0:T(512)S(1)}, f32[512]{0:T(512)}, u32[]{:S(2)}) copy-start(f32[512]{0:T(512)} %get-tuple-element.185) | copy-start | bytes 6148
  931.8 104.8 %copy-start.72 = (f32[512]{0:T(512)S(1)}, f32[512]{0:T(512)}, u32[]{:S(2)}) copy-start(f32[512]{0:T(512)} %get-tuple-element.203) | copy-start | bytes 6148
  1195.5 2.9 copy-start.1
  (41 other events, 59.9 us)
Sparse Core Ops, SparseCore 0:
  9.6 25.2 all-gather.9
  36.5 22.5 all-gather.7
  60.7 22.5 all-gather.11
  84.7 22.5 all-gather.13
  108.7 58.2 all-gather.15
  168.5 58.2 all-gather.17
  228.3 58.2 all-gather.19
  721.4 187.3 reduce-scatter.6
  915.2 279.0 reduce-scatter.8

commit v2 on v1

--- a/solution.py
+++ b/solution.py
@@ -68,7 +68,7 @@
 
 
 def forward_kernel(
-    shape, len_ref, bias_ref, x_ref, *rest
+    shape, len_ref, bias_ref, x_ref, ids_ref, *rest
 ):
     local, head_dim, block, aliased = shape
     if aliased:
@@ -85,7 +85,7 @@
     def _():
         for b in range(count):
             at = pl.ds(b * width, width)
-            row = x_ref[b, 3 * head_dim : 3 * head_dim + 1, :].astype(F32)
+            row = ids_ref[b, 0:1, :].astype(F32)
             extra = key_extra(row, b * width, length, other, same)
             full = jnp.concatenate([x_ref[b, head_dim : 2 * head_dim, :], extra], axis=0)
             keys[at, :] = full.T
@@ -104,7 +104,7 @@
     def _():
         for b in range(sub):
             at = slice(b * width, (b + 1) * width)
-            row = x_ref[step * sub + b, 3 * head_dim : 3 * head_dim + 1, :].astype(F32)
+            row = ids_ref[step * sub + b, 0:1, :].astype(F32)
             query[0:head_dim, at] = x_ref[step * sub + b, 0:head_dim, :]
             query[head_dim:, at] = query_extra(row, (0.0, 0.0, 0.0))
         peak[...] = jnp.full(peak.shape, -FAR, F32)
@@ -153,20 +153,20 @@
         lse_ref[0] = peak[...] + jnp.log2(mass)
 
 
-def attend_forward(x, length, bias, mixed, local, heads_here, head_dim):
+def attend_forward(x, ids, length, bias, mixed, local, heads_here, head_dim):
     count, rows, width = x.shape
     block = max(width, 512)
     seq_len = count * width
     blocks = seq_len // block
     depth = head_dim + EXTRA
     whole = pl.BlockSpec((count, rows, width), lambda i, *_: (0, 0, 0))
-    operands = [length, bias, x]
-    in_specs = [whole]
+    operands = [length, bias, x, ids]
+    in_specs = [whole, pl.BlockSpec((count, AUX, width), lambda i, *_: (0, 3 * head_dim // AUX, 0))]
     aliases = {}
     if mixed is not None:
         operands.append(mixed)
         in_specs.append(pl.BlockSpec(memory_space=pl.ANY))
-        aliases = {3: 0}
+        aliases = {4: 0}
     return pl.pallas_call(
         functools.partial(forward_kernel, (local, head_dim, block, mixed is not None)),
         grid_spec=pltpu.PrefetchScalarGridSpec(
@@ -202,7 +202,7 @@
 
 
 def backward_kernel(
-    shape, len_ref, bias_ref, x_ref, grad_ref, mixed_ref, lse_ref, out_ref, bias_out_ref,
+    shape, len_ref, bias_ref, x_ref, ids_ref, grad_ref, mixed_ref, lse_ref, out_ref, bias_out_ref,
     keys, keys_flat, vals, query, grads, query_rows, grad_rows, acc_keys, acc_vals, acc_query,
 ):
     local, head_dim, block = shape
@@ -218,7 +218,7 @@
         ones = jnp.ones((16, width), BF16)
         for b in range(count):
             at = pl.ds(b * width, width)
-            row = x_ref[b, 3 * head_dim : 3 * head_dim + 1, :].astype(F32)
+            row = ids_ref[b, 0:1, :].astype(F32)
             extra = key_extra(row, b * width, length, other, same)
             here = x_ref[b, head_dim : 2 * head_dim, :]
             keys[at, :] = jnp.concatenate([here, extra], axis=0).T
@@ -240,7 +240,7 @@
         for b in range(sub):
             at = slice(b * width, (b + 1) * width)
             here = step * sub + b
-            row = x_ref[here, 3 * head_dim : 3 * head_dim + 1, :].astype(F32)
+            row = ids_ref[here, 0:1, :].astype(F32)
             shift = pieces(-lse_ref[step][:, at])
             grad = grad_ref[here]
             delta = jnp.sum(grad.astype(F32) * mixed_ref[here].astype(F32), axis=0, keepdims=True)
@@ -283,7 +283,7 @@
         all_total = jnp.zeros((CLASSES, width), F32)
         for b in range(count):
             at = pl.ds(b * width, width)
-            row = x_ref[b, 3 * head_dim : 3 * head_dim + 1, :].astype(F32)
+            row = ids_ref[b, 0:1, :].astype(F32)
             flat = acc_keys[at, :].T
             out_ref[b, head_dim : 2 * head_dim, :] = (flat[0:head_dim] * LN2).astype(BF16)
             out_ref[b, 2 * head_dim : 3 * head_dim, :] = acc_vals[at, :].T[0:head_dim].astype(BF16)
@@ -301,7 +301,7 @@
         bias_out_ref[...] = both
 
 
-def attend_backward(x, grad, mixed, lse, length, bias, local, head_dim):
+def attend_backward(x, ids, grad, mixed, lse, length, bias, local, head_dim):
     count, rows, width = x.shape
     blocks, _, block = lse.shape
     seq_len = count * width
@@ -316,7 +316,11 @@
         grid_spec=pltpu.PrefetchScalarGridSpec(
             num_scalar_prefetch=2,
             grid=(blocks,),
-            in_specs=[whole(x), head_spec, head_spec, whole(lse)],
+            in_specs=[
+                whole(x),
+                pl.BlockSpec((count, AUX, width), lambda i, *_: (0, 3 * head_dim // AUX, 0)),
+                head_spec, head_spec, whole(lse),
+            ],
             out_specs=[
                 pl.BlockSpec((count, 3 * head_dim, width), lambda i, *_: (0, 0, 0)),
                 pl.BlockSpec((8, 128), lambda i, *_: (0, 0)),
@@ -345,7 +349,7 @@
             transcendentals=seq_len * seq_len,
         ),
         name="attend_backward",
-    )(length, bias, x, grad, mixed, lse)
+    )(length, bias, x, ids, grad, mixed, lse)
 
 
 def rotary_tables(places, half_dim):
@@ -354,23 +358,380 @@
     return jnp.cos(angles), jnp.sin(angles)
 
 
-def rotate(values, cosine, sine, reverse):
-    half_dim = values.shape[-2] // 2
-    first = values[..., :half_dim, :]
-    second = values[..., half_dim:, :]
-    if reverse:
-        parts = [first * cosine + second * sine, second * cosine - first * sine]
+def sigmoid_of(x):
+    return 1.0 / (1.0 + jnp.exp2(x * -LOG2E))
+
+
+def project_kernel(
+    shape, tokens_ref, gain_ref, query_ref, key_ref, value_ref, cos_ref, sin_ref, ids_ref, flat_ref, *rest
+):
+    here, head_dim, extras = shape
+    outs, flat_weights = rest[:-1], rest[-1]
+    pair = pl.program_id(0)
+
+    @pl.when(pair == 0)
+    def _():
+        inputs = tokens_ref[0, 0].astype(F32)
+        inverse = lax.rsqrt(jnp.mean(inputs * inputs, axis=-1, keepdims=True) + EPSILON)
+        flat_ref[...] = (inputs * inverse * gain_ref[...]).astype(BF16).T
+
+    flat_weights[0:128, :] = query_ref[...].T
+    flat_weights[128:256, :] = key_ref[...].T
+    flat_weights[256:384, :] = value_ref[...].T
+    made = dot(flat_weights[...], flat_ref[...])
+    cosine, sine = cos_ref[...], sin_ref[...]
+    half = head_dim // 2
+
+    def turned(start, scale):
+        first = made[start : start + half]
+        second = made[start + half : start + head_dim]
+        both = [first * cosine - second * sine, second * cosine + first * sine]
+        return (jnp.concatenate(both, axis=0) * scale).astype(BF16)
+
+    for at in range(128 // head_dim):
+        spot = at * head_dim
+        target, place = (outs[at % here], 0) if here > 1 else (outs[0], at)
+        target[place, 0:head_dim, :] = turned(spot, LOG2E / math.sqrt(head_dim))
+        target[place, head_dim : 2 * head_dim, :] = turned(128 + spot, 1.0)
+        target[place, 2 * head_dim : 3 * head_dim, :] = made[256 + spot : 256 + spot + head_dim].astype(BF16)
+        if extras[at % here]:
+            target[place, 3 * head_dim :, :] = jnp.broadcast_to(ids_ref[...], (AUX, ids_ref.shape[1])).astype(BF16)
+
+
+def project(tokens, unit, gain, weights, cosine, sine, ids, count, here, head_dim):
+    width, model = tokens.shape[2:]
+    heads = count * here
+    pairs = heads * head_dim // 128
+    per = 128 // head_dim // here
+    extras = [h == 0 for h in range(here)]
+
+    def fixed(a):
+        return pl.BlockSpec(a.shape, lambda p: (0,) * a.ndim)
+
+    weight_specs = [pl.BlockSpec((model, 128), lambda p, i=i: (0, i * pairs + p)) for i in range(3)]
+    return pl.pallas_call(
+        functools.partial(project_kernel, (here, head_dim, extras)),
+        grid=(pairs,),
+        in_specs=[
+            pl.BlockSpec((1, 1, width, model), lambda p: unit + (0, 0)),
+            fixed(gain), *weight_specs, fixed(cosine), fixed(sine), fixed(ids),
+        ],
+        out_specs=[pl.BlockSpec((model, width), lambda p: (0, 0))]
+        + [pl.BlockSpec((per, 3 * head_dim + AUX * e, width), lambda p: (p, 0, 0)) for e in extras],
+        out_shape=[jax.ShapeDtypeStruct((model, width), BF16)]
+        + [jax.ShapeDtypeStruct((count, 3 * head_dim + AUX * e, width), BF16) for e in extras],
+        scratch_shapes=[pltpu.VMEM((384, model), BF16)],
+        compiler_params=pltpu.CompilerParams(vmem_limit_bytes=40 << 20),
+        cost_estimate=pl.CostEstimate(
+            flops=6 * width * model * model, bytes_accessed=12 * model * model, transcendentals=0
+        ),
+        name="project",
+    )(tokens, gain, weights, weights, weights, cosine, sine, ids)
+
+
+def middle_kernel(
+    aliased, info_ref, mixed_ref, tokens_ref, cot_ref, out_w_ref, gain_ref, gate_w_ref, up_w_ref, down_w_ref, *rest
+):
+    if aliased:
+        rest = rest[1:]
+    (
+        output_ref, flat_ref, hidden_ref, grad_gate_ref, grad_up_ref, grad_ffn_ref, grad_res_ref,
+        grad_attn_ref, grad_mixed_ref, gain_out_ref, normed, residual, ffn_out, grad_normed,
+    ) = rest
+    step = pl.program_id(0)
+    width = normed.shape[0]
+
+    def valid():
+        index = info_ref[1] + lax.broadcasted_iota(jnp.int32, (width, 1), 0)
+        return jnp.where(index < info_ref[0], 1.0, 0.0)
+
+    def inverse_of(x):
+        return lax.rsqrt(jnp.mean(x * x, axis=-1, keepdims=True) + EPSILON)
+
+    @pl.when(step == 0)
+    def _():
+        inputs = tokens_ref[0, 0].astype(F32) + dot(mixed_ref[...].T, out_w_ref[...])
+        residual[...] = inputs
+        made = (inputs * inverse_of(inputs) * gain_ref[...]).astype(BF16)
+        normed[...] = made
+        flat_ref[...] = made.T
+        grad_ffn_ref[...] = (cot_ref[0, 0].astype(F32) * valid()).astype(BF16)
+        ffn_out[...] = jnp.zeros_like(ffn_out)
+        grad_normed[...] = jnp.zeros_like(grad_normed)
+
+    gate = dot(normed[...], gate_w_ref[...])
+    up = dot(normed[...], up_w_ref[...])
+    grad_hidden = contract(grad_ffn_ref[...], down_w_ref[...], 1, 1)
+    sigmoid = sigmoid_of(gate)
+    silu = gate * sigmoid
+    hidden = (silu * up).astype(BF16)
+    grad_gate = (grad_hidden * up * (sigmoid + silu * (1.0 - sigmoid))).astype(BF16)
+    grad_up = (grad_hidden * silu).astype(BF16)
+    hidden_ref[...] = hidden.T
+    grad_gate_ref[...] = grad_gate
+    grad_up_ref[...] = grad_up
+    ffn_out[...] += dot(hidden, down_w_ref[...])
+    grad_normed[...] += contract(grad_gate, gate_w_ref[...], 1, 1) + contract(grad_up, up_w_ref[...], 1, 1)
+
+    @pl.when(step == pl.num_programs(0) - 1)
+    def _():
+        keep = valid()
+        kept = residual[...]
+        output_ref[0, 0] = ((kept + ffn_out[...]) * keep).astype(BF16)
+        inverse = inverse_of(kept)
+        scaled = grad_normed[...] * gain_ref[...]
+        mean = jnp.mean(scaled * kept, axis=-1, keepdims=True)
+        grad = cot_ref[0, 0].astype(F32) * keep
+        grad = grad + (inverse * scaled - kept * (inverse * inverse * inverse) * mean)
+        gain_out_ref[...] = jnp.sum(grad_normed[...] * kept * inverse, axis=0, keepdims=True)
+        grad_res_ref[...] = grad
+        low = grad.astype(BF16)
+        grad_attn_ref[...] = low
+        grad_mixed_ref[...] = contract(out_w_ref[...], low, 1, 1).astype(BF16)
+
+
+def middle_part(info, mixed, tokens, cotangent, unit, weights, gain, output):
+    width, model = tokens.shape[2:]
+    out_w, gate_w, up_w, down_w = weights
+    ffn = gate_w.shape[1]
+    block = 512
+
+    def fixed(a):
+        return pl.BlockSpec(a.shape, lambda f, *_: (0,) * a.ndim)
+
+    def one(*shape):
+        return pl.BlockSpec(shape, lambda f, *_: (0,) * len(shape))
+
+    token_spec = pl.BlockSpec((1, 1, width, model), lambda f, *_: unit + (0, 0))
+    operands = [info, mixed, tokens, cotangent, out_w, gain, gate_w, up_w, down_w]
+    in_specs = [
+        fixed(mixed), token_spec, token_spec, fixed(out_w), fixed(gain),
+        pl.BlockSpec((model, block), lambda f, *_: (0, f)),
+        pl.BlockSpec((model, block), lambda f, *_: (0, f)),
+        pl.BlockSpec((block, model), lambda f, *_: (f, 0)),
+    ]
+    aliases = {}
+    if output is not None:
+        aliases = {len(operands): 0}
+        operands.append(output)
+        in_specs.append(pl.BlockSpec(memory_space=pl.ANY))
+    struct = jax.ShapeDtypeStruct
+    return pl.pallas_call(
+        functools.partial(middle_kernel, output is not None),
+        grid_spec=pltpu.PrefetchScalarGridSpec(
+            num_scalar_prefetch=1,
+            grid=(ffn // block,),
+            in_specs=in_specs,
+            out_specs=[
+                token_spec, one(model, width),
+                pl.BlockSpec((block, width), lambda f, *_: (f, 0)),
+                pl.BlockSpec((width, block), lambda f, *_: (0, f)),
+                pl.BlockSpec((width, block), lambda f, *_: (0, f)),
+                one(width, model), one(width, model), one(width, model), one(model, width), one(1, model),
+            ],
+            scratch_shapes=[
+                pltpu.VMEM((width, model), BF16),
+                pltpu.VMEM((width, model), F32),
+                pltpu.VMEM((width, model), F32),
+                pltpu.VMEM((width, model), F32),
+            ],
+        ),
+        out_shape=[
+            struct(tokens.shape, BF16), struct((model, width), BF16), struct((ffn, width), BF16),
+            struct((width, ffn), BF16), struct((width, ffn), BF16), struct((width, model), BF16),
+            struct((width, model), F32), struct((width, model), BF16), struct((model, width), BF16),
+            struct((1, model), F32),
+        ],
+        input_output_aliases=aliases,
+        compiler_params=pltpu.CompilerParams(vmem_limit_bytes=62 << 20),
+        cost_estimate=pl.CostEstimate(
+            flops=12 * width * model * ffn, bytes_accessed=8 * model * ffn, transcendentals=width * ffn
+        ),
+        name="middle_part",
+    )(*operands)
+
+
+def weights_kernel(units, *refs):
+    out_ref = refs[-1]
+    total = dot(refs[0][...], refs[units][...])
+    for u in range(1, units):
+        total += dot(refs[u][...], refs[units + u][...])
+    out_ref[...] = total.astype(BF16).reshape(out_ref.shape)
+
+
+def weight_grad(lefts, rights, by_left, out_struct, out_spec, steps, into, name):
+    units = len(lefts)
+
+    def fixed(a):
+        return pl.BlockSpec(a.shape, lambda n: (0, 0))
+
+    def left_spec(a):
+        return pl.BlockSpec((a.shape[0] // steps, a.shape[1]), lambda n: (n, 0))
+
+    def right_spec(a):
+        return pl.BlockSpec((a.shape[0], a.shape[1] // steps), lambda n: (0, n))
+
+    operands = list(lefts) + list(rights)
+    if by_left:
+        in_specs = [left_spec(a) for a in lefts] + [fixed(a) for a in rights]
     else:
-        parts = [first * cosine - second * sine, second * cosine + first * sine]
-    return jnp.concatenate(parts, axis=-2)
-
-
-def norm_back(grad_normed, inputs, inverse, gain):
-    scaled = grad_normed * gain
-    grad_inputs = inverse * scaled - inputs * (inverse * inverse * inverse) * jnp.mean(
-        scaled * inputs, axis=-1, keepdims=True
+        in_specs = [fixed(a) for a in lefts] + [right_spec(a) for a in rights]
+    aliases = {}
+    if into is not None:
+        aliases = {len(operands): 0}
+        operands.append(into)
+        in_specs.append(pl.BlockSpec(memory_space=pl.ANY))
+    return pl.pallas_call(
+        functools.partial(weights_kernel, units),
+        grid=(steps,),
+        in_specs=in_specs,
+        out_specs=out_spec,
+        out_shape=out_struct,
+        input_output_aliases=aliases,
+        compiler_params=pltpu.CompilerParams(vmem_limit_bytes=48 << 20),
+        cost_estimate=pl.CostEstimate(
+            flops=2 * units * lefts[0].shape[0] * lefts[0].shape[1] * rights[0].shape[1],
+            bytes_accessed=2 * lefts[0].shape[0] * rights[0].shape[1],
+            transcendentals=0,
+        ),
+        name=name,
+    )(*operands)
+
+
+def final_kernel(
+    shape, tokens_ref, grad_res_ref, gain_ref, query_ref, key_ref, value_ref, cos_ref, sin_ref, *rest
+):
+    here, head_dim, aliased = shape
+    back = rest[:here]
+    rest = rest[here:]
+    if aliased:
+        rest = rest[1:]
+    out_ref, grad_q_ref, grad_k_ref, grad_v_ref, gain_out_ref, total = rest
+    step = pl.program_id(0)
+    cosine, sine = cos_ref[...], sin_ref[...]
+    half = head_dim // 2
+
+    def turned(x):
+        first, second = x[:half].astype(F32), x[half:].astype(F32)
+        return jnp.concatenate(
+            [first * cosine + second * sine, second * cosine - first * sine], axis=0
+        ).astype(BF16)
+
+    for at in range(256 // head_dim):
+        place = slice(at * head_dim, (at + 1) * head_dim)
+        part = back[at % here]
+        grad_q_ref[place, :] = turned(part[at // here, 0:head_dim, :])
+        grad_k_ref[place, :] = turned(part[at // here, head_dim : 2 * head_dim, :])
+        grad_v_ref[place, :] = part[at // here, 2 * head_dim : 3 * head_dim, :]
+    made = (
+        contract(grad_q_ref[...].T, query_ref[...], 1, 1)
+        + contract(grad_k_ref[...].T, key_ref[...], 1, 1)
+        + contract(grad_v_ref[...].T, value_ref[...], 1, 1)
     )
-    return grad_inputs, jnp.sum(grad_normed * inputs * inverse, axis=0)
+
+    @pl.when(step == 0)
+    def _():
+        total[...] = made
+
+    @pl.when(step > 0)
+    def _():
+        total[...] += made
+
+    @pl.when(step == pl.num_programs(0) - 1)
+    def _():
+        inputs = tokens_ref[0, 0].astype(F32)
+        inverse = lax.rsqrt(jnp.mean(inputs * inputs, axis=-1, keepdims=True) + EPSILON)
+        scaled = total[...] * gain_ref[...]
+        mean = jnp.mean(scaled * inputs, axis=-1, keepdims=True)
+        grad = inverse * scaled - inputs * (inverse * inverse * inverse) * mean
+        out_ref[0, 0] = (grad_res_ref[...] + grad).astype(BF16)
+        gain_out_ref[...] = jnp.sum(total[...] * inputs * inverse, axis=0, keepdims=True)
+
+
+def final_part(tokens, unit, grad_res, gain, weights, cosine, sine, back, head_dim, output):
+    width, model = tokens.shape[2:]
+    here = len(back)
+    steps = model // 256
+
+    def fixed(a):
+        return pl.BlockSpec(a.shape, lambda c: (0,) * a.ndim)
+
+    token_spec = pl.BlockSpec((1, 1, width, model), lambda c: unit + (0, 0))
+    weight_specs = [pl.BlockSpec((model, 256), lambda c, i=i: (0, i * steps + c)) for i in range(3)]
+    row_spec = pl.BlockSpec((256, width), lambda c: (c, 0))
+    operands = [tokens, grad_res, gain, weights, weights, weights, cosine, sine, *back]
+    in_specs = [
+        token_spec, fixed(grad_res), fixed(gain), *weight_specs,
+        fixed(cosine), fixed(sine),
+    ] + [
+        pl.BlockSpec((256 // head_dim // here, 3 * head_dim, width), lambda c: (c, 0, 0)) for _ in back
+    ]
+    aliases = {}
+    if output is not None:
+        aliases = {len(operands): 0}
+        operands.append(output)
+        in_specs.append(pl.BlockSpec(memory_space=pl.ANY))
+    struct = jax.ShapeDtypeStruct
+    return pl.pallas_call(
+        functools.partial(final_kernel, (here, head_dim, output is not None)),
+        grid=(steps,),
+        in_specs=in_specs,
+        out_specs=[token_spec, row_spec, row_spec, row_spec, pl.BlockSpec((1, model), lambda c: (0, 0))],
+        out_shape=[
+            struct(tokens.shape, BF16), struct((model, width), BF16), struct((model, width), BF16),
+            struct((model, width), BF16), struct((1, model), F32),
+        ],
+        scratch_shapes=[pltpu.VMEM((width, model), F32)],
+        input_output_aliases=aliases,
+        compiler_params=pltpu.CompilerParams(vmem_limit_bytes=48 << 20),
+        cost_estimate=pl.CostEstimate(
+            flops=6 * width * model * model, bytes_accessed=12 * model * model, transcendentals=0
+        ),
+        name="final_part",
+    )(*operands)
+
+
+def attn_weights_kernel(units, *refs):
+    left = refs[0:units]
+    mixed = refs[units : 2 * units]
+    cols = [refs[(2 + i) * units : (3 + i) * units] for i in range(4)]
+    outs = refs[6 * units :]
+    for i in range(4):
+        total = None
+        for u in range(units):
+            if i < 3:
+                part = contract(left[u][...], cols[i][u][...], 1, 1)
+            else:
+                part = dot(mixed[u][...], cols[i][u][...])
+            total = part if total is None else total + part
+        outs[i][...] = total.astype(BF16)
+
+
+def attn_weight_grads(lefts, mixed, queries, keys, values, grad_attn):
+    units = len(lefts)
+    model, width = lefts[0].shape
+    block = 256
+
+    def fixed(a):
+        return pl.BlockSpec(a.shape, lambda c: (0, 0))
+
+    in_specs = [fixed(a) for a in lefts] + [fixed(a) for a in mixed]
+    for _ in range(3 * units):
+        in_specs.append(pl.BlockSpec((block, width), lambda c: (c, 0)))
+    for _ in range(units):
+        in_specs.append(pl.BlockSpec((width, block), lambda c: (0, c)))
+    return pl.pallas_call(
+        functools.partial(attn_weights_kernel, units),
+        grid=(model // block,),
+        in_specs=in_specs,
+        out_specs=[pl.BlockSpec((model, block), lambda c: (0, c))] * 4,
+        out_shape=[jax.ShapeDtypeStruct((model, model), BF16)] * 4,
+        compiler_params=pltpu.CompilerParams(vmem_limit_bytes=48 << 20),
+        cost_estimate=pl.CostEstimate(
+            flops=8 * units * width * model * model, bytes_accessed=8 * model * model, transcendentals=0
+        ),
+        name="attn_weight_grads",
+    )(*lefts, *mixed, *queries, *keys, *values, *grad_attn)
 
 
 def on_device(
@@ -383,10 +744,11 @@
     count = lax.axis_size("seq")
     here = heads // count
     ffn = w_gate.shape[1]
+    devices = lax.axis_size("shard") * count
     seq_index = lax.axis_index("seq")
     bias_here = lax.dynamic_slice_in_dim(bias_table, seq_index * here, here, 0)
-    row_index = seq_index * width + jnp.arange(width, dtype=jnp.int32)
     units = [(m, s) for m in range(micro) for s in range(seqs)]
+    attn_row, ffn_row = attn_gain[None, :], ffn_gain[None, :]
 
     def gather(weight):
         return lax.all_gather(weight, "shard", axis=0, tiled=True)
@@ -394,152 +756,220 @@
     def exchange(values):
         return lax.all_to_all(values, "seq", split_axis=0, concat_axis=0, tiled=True)
 
-    query_full, key_full, value_full = gather(w_query), gather(w_key), gather(w_value)
-    out_full, gate_full, up_full, down_full = (
-        gather(w_out), gather(w_gate), gather(w_up), gather(w_down)
+    def after(value, *before):
+        return lax.optimization_barrier((value,) + before)[0]
+
+    attn_joined = gather(jnp.concatenate([w_query, w_key, w_value], axis=1))
+    ffn_weights = [gather(w_out), gather(w_gate), gather(w_up), gather(w_down)]
+
+    packed_list, flats, tables = [], [], []
+
+    def run_project(u, token):
+        m, s = units[u]
+        cosine, sine = rotary_tables(positions[m, s], head_dim // 2)
+        ids = after(variates[m, s].astype(F32)[None, :], *token)
+        flat, *packed = project(
+            tokens, (m, s), attn_row, attn_joined, cosine, sine, ids, count, here, head_dim
+        )
+        flats.append(flat)
+        tables.append((cosine, sine))
+        packed_list.append(packed)
+
+    sent = {}
+    mixed_now = [None] * len(units)
+    sums = {}
+    mixed_tok = {}
+    middle = [None] * len(units)
+    grad_heads = {}
+    state = {"output": None, "grads": None}
+    packed_grads = {}
+    returned = {}
+    bias_terms = {}
+    finals = [None] * len(units)
+
+    def length_of(u, token):
+        m, s = units[u]
+        return after(lengths[m, s].reshape(1), *token)
+
+    def run_forward(u, h, token):
+        mixed_now[u], sums[u, h] = attend_forward(
+            sent[u, h], sent[u, 0], length_of(u, token), bias_here, mixed_now[u], h, here, head_dim
+        )
+        return sums[u, h]
+
+    def run_middle(u, token):
+        m, s = units[u]
+        info = jnp.stack([lengths[m, s], seq_index * width]).astype(jnp.int32)
+        state["output"], *middle[u] = middle_part(
+            after(info, *token), mixed_tok[u], tokens, cotangent, (m, s), ffn_weights, ffn_row,
+            state["output"],
+        )
+        return middle[u][8]
+
+    def run_backward(u, h, token):
+        packed_grads[u, h], both = attend_backward(
+            sent[u, h], sent[u, 0], grad_heads[u], mixed_now[u], sums[u, h], length_of(u, token),
+            bias_here, h, head_dim,
+        )
+        bias_terms[u, h] = jnp.stack([both[1, 0] - both[0, 0], both[0, 0]])
+        return both
+
+    def run_final(u, token):
+        m, s = units[u]
+        cosine, sine = tables[u]
+        state["grads"], *finals[u] = final_part(
+            tokens, (m, s), middle[u][5], after(attn_row, *token), attn_joined, cosine, sine,
+            [returned[u, h] for h in range(here)], head_dim, state["grads"],
+        )
+        return finals[u][3]
+
+    rows = model // devices
+    fold = ffn // model
+    part = ffn // fold
+
+    def run_weights(token):
+        if rows % 16:
+
+            def plain(left, right):
+                total = sum(dot(item[left], item[right]) for item in middle)
+                return total.astype(BF16)
+
+            def spread(total):
+                split = total.reshape(devices, rows, fold, part)
+                return jnp.swapaxes(split, 1, 2).reshape(ffn, part)
+
+            return jnp.concatenate([plain(1, 4), spread(plain(0, 2)), spread(plain(0, 3))], axis=1)
+        struct = jax.ShapeDtypeStruct((devices, fold, rows, 3 * part), BF16)
+        block = 512
+        per = part // block
+        down = pl.BlockSpec((block // (fold * rows), fold, rows, model), lambda n: (n, 0, 0, 0))
+        gate = pl.BlockSpec((devices, 1, rows, block), lambda n: (0, n // per, 0, per + n % per))
+        up = pl.BlockSpec((devices, 1, rows, block), lambda n: (0, n // per, 0, 2 * per + n % per))
+        steps = ffn // block
+        lefts = [item[0] for item in middle]
+        firsts = [after(middle[0][4], *token)] + [item[4] for item in middle[1:]]
+        terms = weight_grad(
+            [item[1] for item in middle], firsts, True, struct, down, steps, None, "down_grad"
+        )
+        terms = weight_grad(
+            lefts, [item[2] for item in middle], False, struct, gate, steps, terms, "gate_grad"
+        )
+        terms = weight_grad(
+            lefts, [item[3] for item in middle], False, struct, up, steps, terms, "up_grad"
+        )
+        return terms.reshape(ffn, 3 * part)
+
+    holder = {}
+
+    def weights_work(token):
+        holder["terms"] = run_weights(token)
+        return holder["terms"]
+
+    def send_packed(u, h):
+        def keep(moved):
+            sent[u, h] = moved
+
+        return lambda: packed_list[u][h], keep
+
+    def send_mixed(u):
+        def keep(moved):
+            mixed_tok[u] = moved.reshape(model, width)
+
+        return lambda: mixed_now[u], keep
+
+    def send_heads(u):
+        def keep(moved):
+            grad_heads[u] = moved
+
+        return lambda: middle[u][7].reshape(count, here * head_dim, width), keep
+
+    def send_back(u, h):
+        def keep(moved):
+            returned[u, h] = moved
+
+        return lambda: packed_grads[u, h], keep
+
+    def work_project(u):
+        def work(token):
+            run_project(u, token)
+            return flats[u]
+
+        return work
+
+    def work(function, *args):
+        return lambda token: function(*args, token)
+
+    total = len(units)
+    order = [(u, h) for u in range(total) for h in range(here)]
+    if total == 2 and here == 2:
+        steps = [
+            (work_project(0), None),
+            (work_project(1), send_packed(0, 0)),
+            (work(run_forward, 0, 0), send_packed(0, 1)),
+            (work(run_forward, 0, 1), send_packed(1, 0)),
+            (work(run_forward, 1, 0), send_mixed(0)),
+            (work(run_middle, 0), send_packed(1, 1)),
+            (work(run_forward, 1, 1), send_heads(0)),
+            (work(run_backward, 0, 0), send_mixed(1)),
+            (work(run_middle, 1), send_back(0, 0)),
+            (weights_work, send_heads(1)),
+            (work(run_backward, 0, 1), None),
+            (work(run_backward, 1, 0), send_back(0, 1)),
+            (work(run_backward, 1, 1), send_back(1, 0)),
+            (work(run_final, 0), send_back(1, 1)),
+            (work(run_final, 1), None),
+        ]
+    else:
+        steps = [(work_project(u), None) for u in range(total)]
+        steps += [(None, send_packed(*at)) for at in order]
+        for u in range(total):
+            steps += [(work(run_forward, u, h), None) for h in range(here)]
+            steps += [(None, send_mixed(u))]
+        for u in range(total):
+            steps += [(work(run_middle, u), None), (None, send_heads(u))]
+        steps += [(weights_work, None)]
+        for at in order:
+            steps += [(work(run_backward, *at), None), (None, send_back(*at))]
+        steps += [(work(run_final, u), None) for u in range(total)]
+
+    token = ()
+    for task, send in steps:
+        done = ()
+        moved = None
+        if send is not None:
+            moved = exchange(after(send[0](), *token))
+            done = (moved,)
+        if task is not None:
+            done = done + (task(token),)
+        if send is not None:
+            send[1](moved)
+        token = done
+    ffn_owned = lax.psum_scatter(holder["terms"], ("shard", "seq"), scatter_dimension=0, tiled=True)
+    acc_bias = sum(jnp.stack([bias_terms[u, h] for h in range(here)]) for u in range(len(units)))
+    attn_terms = attn_weight_grads(
+        flats, [mixed_tok[u] for u in range(len(units))],
+        [item[0] for item in finals], [item[1] for item in finals], [item[2] for item in finals],
+        [item[6] for item in middle],
     )
-
-    first = []
-    for m, s in units:
-        inputs = tokens[m, s].astype(F32)
-        inverse = lax.rsqrt(jnp.mean(inputs * inputs, axis=-1, keepdims=True) + EPSILON)
-        normed = (inputs * inverse * attn_gain).astype(BF16)
-        cosine, sine = rotary_tables(positions[m, s], head_dim // 2)
-
-        def project(weight):
-            return contract(weight, normed, 0, 1).reshape(heads, head_dim, width)
-
-        scale = LOG2E / math.sqrt(head_dim)
-        query = (rotate(project(query_full), cosine, sine, False) * scale).astype(BF16)
-        key = rotate(project(key_full), cosine, sine, False).astype(BF16)
-        value = project(value_full).astype(BF16)
-        extra = jnp.broadcast_to(variates[m, s].astype(BF16)[None, None, :], (heads, AUX, width))
-        packed = jnp.concatenate([query, key, value, extra], axis=1)
-        packed = packed.reshape(count, here, 3 * head_dim + AUX, width)
-        sent = [exchange(packed[:, h]) for h in range(here)]
-        first.append((normed, inverse, cosine, sine, sent))
-
-    attended = []
-    for (m, s), item in zip(units, first):
-        sent = item[4]
-        length = lengths[m, s].reshape(1)
-        mixed = None
-        sums = []
-        for h in range(here):
-            mixed, lse = attend_forward(sent[h], length, bias_here, mixed, h, here, head_dim)
-            sums.append(lse)
-        mixed_tok = exchange(mixed).reshape(model, width)
-        attended.append((mixed, sums, mixed_tok))
-
-    outputs = [[None] * seqs for _ in range(micro)]
-    middle = []
-    acc_ffn_gain = jnp.zeros((model,), F32)
-    for (m, s), (mixed, sums, mixed_tok) in zip(units, attended):
-        valid = (row_index < lengths[m, s]).astype(F32)[:, None]
-        inputs = tokens[m, s].astype(F32)
-        residual = inputs + contract(mixed_tok, out_full, 0, 0)
-        inverse = lax.rsqrt(jnp.mean(residual * residual, axis=-1, keepdims=True) + EPSILON)
-        normed = (residual * inverse * ffn_gain).astype(BF16)
-        gate = dot(normed, gate_full)
-        up = dot(normed, up_full)
-        sigmoid = jax.nn.sigmoid(gate)
-        silu = gate * sigmoid
-        hidden = (silu * up).astype(BF16)
-        outputs[m][s] = ((residual + dot(hidden, down_full)) * valid).astype(BF16)
-        masked = cotangent[m, s].astype(F32) * valid
-        grad_ffn = masked.astype(BF16)
-        grad_hidden = contract(grad_ffn, down_full, 1, 1)
-        grad_gate = (grad_hidden * up * (sigmoid + silu * (1.0 - sigmoid))).astype(BF16)
-        grad_up = (grad_hidden * silu).astype(BF16)
-        grad_normed = contract(grad_gate, gate_full, 1, 1) + contract(grad_up, up_full, 1, 1)
-        grad_res, gain_term = norm_back(grad_normed, residual, inverse, ffn_gain)
-        acc_ffn_gain = acc_ffn_gain + gain_term
-        grad_residual = masked + grad_res
-        grad_attn = grad_residual.astype(BF16)
-        grad_mixed = contract(out_full, grad_attn, 1, 1).astype(BF16)
-        grad_heads = exchange(grad_mixed.reshape(count, here * head_dim, width))
-        middle.append((normed, hidden, grad_ffn, grad_gate, grad_up, grad_residual, grad_attn, grad_heads))
-
-    def joined(parts):
-        return parts[0] if len(parts) == 1 else jnp.concatenate(parts, axis=0)
-
-    normed_all = joined([item[0] for item in middle])
-    hidden_all = joined([item[1] for item in middle])
-    ffn_all = joined([item[2] for item in middle])
-    devices = lax.axis_size("shard") * count
-    rows = model // devices
-    down_rows = ffn // devices
-    fold = down_rows // rows
-
-    def spread(total):
-        split = total.reshape(devices, rows, fold, ffn // fold)
-        return jnp.swapaxes(split, 1, 2).reshape(ffn, ffn // fold)
-
-    gate_term = contract(normed_all, joined([item[3] for item in middle]), 0, 0).astype(BF16)
-    up_term = contract(normed_all, joined([item[4] for item in middle]), 0, 0).astype(BF16)
-    down_term = contract(hidden_all, ffn_all, 0, 0).astype(BF16)
-    ffn_terms = jnp.concatenate([down_term, spread(gate_term), spread(up_term)], axis=1)
-    ffn_owned = lax.psum_scatter(ffn_terms, ("shard", "seq"), scatter_dimension=0, tiled=True)
-
-    grads = [[None] * seqs for _ in range(micro)]
-    acc_attn_gain = jnp.zeros((model,), F32)
-    acc_bias = jnp.zeros((here, 2), F32)
-    returned = []
-    for (m, s), before, (mixed, sums, _), item in zip(units, first, attended, middle):
-        sent = before[4]
-        length = lengths[m, s].reshape(1)
-        back = []
-        terms = []
-        for h in range(here):
-            packed, both = attend_backward(
-                sent[h], item[7], mixed, sums[h], length, bias_here, h, head_dim
-            )
-            back.append(exchange(packed))
-            terms.append(jnp.stack([both[1, 0] - both[0, 0], both[0, 0]]))
-        acc_bias = acc_bias + jnp.stack(terms)
-        returned.append(back)
-    for (m, s), before, item, back in zip(units, first, middle, returned):
-        normed, inverse, cosine, sine, _ = before
-        grad_residual = item[5]
-        full = jnp.stack(back, axis=1).reshape(heads, 3, head_dim, width)
-        grad_q = rotate(full[:, 0].astype(F32), cosine, sine, True).astype(BF16).reshape(model, width)
-        grad_k = rotate(full[:, 1].astype(F32), cosine, sine, True).astype(BF16).reshape(model, width)
-        grad_v = full[:, 2].reshape(model, width)
-        grad_normed = (
-            contract(grad_q, query_full, 0, 1)
-            + contract(grad_k, key_full, 0, 1)
-            + contract(grad_v, value_full, 0, 1)
-        )
-        inputs = tokens[m, s].astype(F32)
-        grad_in, gain_term = norm_back(grad_normed, inputs, inverse, attn_gain)
-        acc_attn_gain = acc_attn_gain + gain_term
-        grads[m][s] = (grad_residual + grad_in).astype(BF16)
-        returned[m * seqs + s] = (grad_q, grad_k, grad_v)
-
-    attn_normed = joined([item[0] for item in first])
-    grad_cols = [jnp.concatenate([item[i] for item in returned], axis=1) for i in range(3)]
-    terms = [contract(attn_normed, cols, 0, 1) for cols in grad_cols]
-    mixed_cols = jnp.concatenate([item[2] for item in attended], axis=1)
-    terms.append(contract(mixed_cols, joined([item[6] for item in middle]), 1, 0))
     pad = (-(4 * model)) % 384
-    attn_terms = jnp.concatenate(terms + [jnp.zeros((model, pad), F32)], axis=1).astype(BF16)
+    attn_terms = jnp.concatenate([*attn_terms, jnp.zeros((model, pad), BF16)], axis=1)
     attn_owned = lax.psum_scatter(attn_terms, ("shard", "seq"), scatter_dimension=0, tiled=True)
 
     bias_full = lax.dynamic_update_slice(
         jnp.zeros((heads, 2), F32), acc_bias, (seq_index * here, jnp.int32(0))
     )
     grad_attn_gain, grad_ffn_gain, grad_bias = lax.psum(
-        (acc_attn_gain, acc_ffn_gain, bias_full), ("shard", "seq")
+        (sum(item[3][0] for item in finals), sum(item[8][0] for item in middle), bias_full),
+        ("shard", "seq"),
     )
 
-    def unspread(part):
-        return jnp.swapaxes(part.reshape(fold, rows, ffn // fold), 0, 1).reshape(rows, ffn).astype(F32)
-
-    part = ffn // fold
+    def unspread(owned):
+        return jnp.swapaxes(owned.reshape(fold, rows, part), 0, 1).reshape(rows, ffn).astype(F32)
+
     attn_owned = attn_owned.astype(F32)
     return (
-        jnp.stack([jnp.stack(item) for item in outputs]),
-        jnp.stack([jnp.stack(item) for item in grads]),
+        state["output"],
+        state["grads"],
         grad_attn_gain,
         attn_owned[:, 0:model],
         attn_owned[:, model : 2 * model],

time: 1210 us -> 1100 us (0.909)
  matrix products: 245 us -> 0 us
  Pallas kernels: 145 us -> 364 us
  waiting for transfers between devices: 409 us -> 536 us
  local copies, waits for them, and re-layouts: 173 us -> 49.5 us
  other arithmetic: 56 us -> 10.5 us
  blocking collectives: 101 us -> 58.1 us
    dot_general x35 -> x0, matrix products: 245 us -> none  [the longest x29 183 us: contract(): lax.dot_general(a, b, (((da,), (db,)), ((), ())), preferred_element_type=...]
    reduce_scatter x1 -> x2, waiting for transfers between devices: 147 us -> 331 us  [the longest x1 249 us: on_device(): lax.psum_scatter(holder['terms'], ('shard', 'seq'), scatter_dimension=0,...]
    pallas_call x0 -> x10, Pallas kernels: none -> 173 us  [the longest x2 83.7 us: middle_part(): pl.pallas_call(functools.partial(middle_kernel, output is not None), grid...]
    reshape x6 -> x0, local copies, waits for them, and re-layouts: 73.4 us -> none  [the longest x4 50.5 us: spread(): split = total.reshape(devices, rows, fold, ffn // fold)]
    all_to_all x12, waiting for transfers between devices: 204 us -> 133 us  [exchange(): lax.all_to_all(values, 'seq', split_axis=0, concat_axis=0, tiled=True)]
    psum x1, blocking collectives: 101 us -> 58.1 us  [on_device(): lax.psum((sum((item[3][0] for item in finals)), sum((item[8][0] for item...]
    pallas_call x4, Pallas kernels: 95.1 us -> 123 us  [attend_backward(): pl.pallas_call(functools.partial(backward_kernel, (local, head_dim, block...]
    unnamed x184 -> x119, local copies, waits for them, and re-layouts: 70.3 us -> 42.5 us
  transfers between devices with their start and end apart: 21 -> 19, of which waited for: 16 -> 12; matrix products, arithmetic and copies ran while one was open for 26% -> 1% of each run, Pallas kernels for 12% -> 26%
where the time goes in v2:
time: 1100 us
  waiting for transfers between devices  536 us (49%)
  Pallas kernels  364 us (33%)
  starting transfers between devices  61.6 us (6%)
  blocking collectives  58.1 us (5%)
  local copies, waits for them, and re-layouts  49.5 us (4%)
  between operations  20.4 us (2%)
    reduce_scatter x1, waiting for transfers between devices, on_device(): lax.psum_scatter(holder['terms'], ('shard', 'seq'), scatter_dimension=0,...  249 us
    all_to_all x12, waiting for transfers between devices, exchange(): lax.all_to_all(values, 'seq', split_axis=0, concat_axis=0, tiled=True)  133 us
    pallas_call x4, Pallas kernels, attend_backward(): pl.pallas_call(functools.partial(backward_kernel, (local, head_dim, block...  123 us
    pallas_call x2, Pallas kernels, middle_part(): pl.pallas_call(functools.partial(middle_kernel, output is not None), grid...  83.7 us
    reduce_scatter x1, waiting for transfers between devices, on_device(): lax.psum_scatter(attn_terms, ('shard', 'seq'), scatter_dimension=0, tiled...  81.7 us
    all_gather x5, waiting for transfers between devices, gather(): return lax.all_gather(weight, 'shard', axis=0, tiled=True)  68.7 us
    pallas_call x4, Pallas kernels, attend_forward(): pl.pallas_call(functools.partial(forward_kernel, (local, head_dim, block,...  67.8 us
    all_to_all x12, starting transfers between devices, exchange(): lax.all_to_all(values, 'seq', split_axis=0, concat_axis=0, tiled=True)  61.3 us
  transfers between devices with their start and end apart: 19, of which 12 were waited for; matrix products, arithmetic and copies ran while one was open for 1% of the time, Pallas kernels for 26%

profile of v2, /device:TPU:0, one launch (start us, length us, event | category | flops | bytes accessed | tf_op | source)
XLA Modules:
  0.0 1099.6 jit_solution(9307360506834918247)
XLA Ops:
  7.2 2.6 pad_maximum_fusion
  12.6 46.7 %all-gather.6.cloned.1.call-done.query_ref.key_ref.value_ref = bf16[1024,3072]{1,0:T(8,128)(2,1)} async-done(((bf16[256,3072]{1,0:T(8,128)(2,1)}), bf16[1024,3072]{1,0:T(8,128)(2,1)}) %all-gather.6.cloned.1.call-update) | async-done | bytes 6291472 | tf_op jit(solution)/shard_map/all_gather | solution.py:754
  59.3 2.8 copy-done.2
  62.1 1.6 copy-done.4
  63.7 7.4 project.2
  71.1 1.2 copy-done.9
  72.3 1.2 copy-done.12
  74.5 5.6 all-to-all-start
  81.5 2.8 copy-done.3
  84.3 1.6 copy-done.5
  85.9 7.4 project.3
  93.3 1.2 copy-done.10
  95.6 24.8 %all-to-all-done.x_ref.ids_ref = bf16[8,208,512]{2,1,0:T(8,128)(2,1)S(1)} async-done(((bf16[8,208,512]{2,1,0:T(8,128)(2,1)}), bf16[8,208,512]{2,1,0:T(8,128)(2,1)S(1)}, u32[]{:S(2)}, u32[]{:S(2)}) %all-to-all-start) | async-done | bytes 1703968 | tf_op jit(solution)/shard_map/all_to_all | solution.py:757
  120.3 4.3 all-to-all-start.1
  124.6 25.8 %attend_forward.4 = (bf16[8,128,512]{2,1,0:T(8,128)(2,1)}, f32[8,1,512]{2,1,0:T(1,128)S(1)}) custom-call(s32[1]{0:T(128)} %bitcast.7.len_ref, f32[2,2]{1,0:T(2,128)S(1)} %copy.37.bias_ref, bf16[8,208,512]{2,1,0:T(8,128)(2,1)S(1)} %all-to-all-done.x_ref.ids_ref, bf16[8,208,512]{2,1,0:T(8,128)(2,1)S(1)} %all-to-all-done.x_ref.ids_ref), custom_call_target="tpu_custom_call" | custom-call | flops 34359738368 | bytes 3407872 | tf_op jit(solution)/shard_map/attend_forward/pallas_call | solution.py:170
  150.5 10.8 all-to-all-done.1.x_ref
  161.3 4.3 all-to-all-start.2
  165.6 27.2 %attend_forward.5 = (bf16[8,128,512]{2,1,0:T(8,128)(2,1)}, f32[8,1,512]{2,1,0:T(1,128)S(1)}) custom-call(s32[1]{0:T(128)} %bitcast.7.len_ref, f32[2,2]{1,0:T(2,128)S(1)} %copy.37.bias_ref, bf16[8,192,512]{2,1,0:T(8,128)(2,1)} %all-to-all-done.1.x_ref, bf16[8,208,512]{2,1,0:T(8,128)(2,1)S(1)} %all-to-all-done.x_ref.ids_ref, ...), custom_call_target="tpu_custom_call", output_to_operand_aliasing={{0}: (4, {})} | custom-call | flops 34359738368 | bytes 3145728 | tf_op jit(solution)/shard_map/attend_forward/pallas_call | solution.py:170
  192.8 12.2 %all-to-all-done.2.x_ref.ids_ref = bf16[8,208,512]{2,1,0:T(8,128)(2,1)} async-done(((bf16[8,208,512]{2,1,0:T(8,128)(2,1)}), bf16[8,208,512]{2,1,0:T(8,128)(2,1)}, u32[]{:S(2)}, u32[]{:S(2)}) %all-to-all-start.2) | async-done | bytes 1703968 | tf_op jit(solution)/shard_map/all_to_all | solution.py:757
  205.0 4.2 all-to-all-start.3
  209.3 7.5 attend_forward.6
  217.8 17.1 %all-to-all-done.3 = bf16[8,128,512]{2,1,0:T(8,128)(2,1)} async-done(((bf16[8,128,512]{2,1,0:T(8,128)(2,1)}), bf16[8,128,512]{2,1,0:T(8,128)(2,1)}, u32[]{:S(2)}, u32[]{:S(2)}) %all-to-all-start.3) | async-done | bytes 1048608 | tf_op jit(solution)/shard_map/all_to_all | solution.py:757
  234.9 4.8 all-to-all-start.4
  239.7 1.2 pad_add_fusion.1.info_ref
  240.9 22.0 %all-gather.14.cloned.1.call-done.down_w_ref = bf16[4096,1024]{1,0:T(8,128)(2,1)} async-done(((bf16[1024,1024]{1,0:T(8,128)(2,1)}), bf16[4096,1024]{1,0:T(8,128)(2,1)}) %all-gather.14.cloned.1.call-update) | async-done | bytes 8388624 | tf_op jit(solution)/shard_map/all_gather | solution.py:754
  262.9 41.9 %middle_part.2 = (bf16[2,1,512,1024]{3,2,1,0:T(8,128)(2,1)}, bf16[1024,512]{1,0:T(8,128)(2,1)}, bf16[4096,512]{1,0:T(8,128)(2,1)}, bf16[512,4096]{1,0:T(8,128)(2...) custom-call(s32[2]{0:T(128)} %pad_add_fusion.1.info_ref, ...), custom_call_target="tpu_custom_call" | custom-call | flops 25769803776 | bytes 33554432 | tf_op jit(solution)/shard_map/middle_part/pallas_call | solution.py:519
  304.8 5.6 all-to-all-start.5
  310.3 1.2 copy-done.25
  311.5 7.3 attend_forward.7
  319.8 16.7 %all-to-all-done.5.grad_ref = bf16[8,128,512]{2,1,0:T(8,128)(2,1)S(1)} async-done(((bf16[8,128,512]{2,1,0:T(8,128)(2,1)}), bf16[8,128,512]{2,1,0:T(8,128)(2,1)S(1)}, u32[]{:S(2)}, u32[]{:S(2)}) %all-to-all-start.5) | async-done | bytes 1048608 | tf_op jit(solution)/shard_map/all_to_all | solution.py:757
  337.6 3.8 all-to-all-start.6
  341.4 1.2 copy-done.22
  342.6 49.5 %attend_backward.4 = (bf16[8,192,512]{2,1,0:T(8,128)(2,1)S(1)}, f32[8,128]{1,0:T(8,128)S(1)}) custom-call(s32[1]{0:T(128)} %bitcast.7.len_ref, f32[2,2]{1,0:T(2,128)S(1)} %copy.37.bias_ref, bf16[8,208,512]{2,1,0:T(8,128)(2,1)S(1)} %all-to-all-done.x_ref.ids_ref, bf16[8,208,512]{2,1,0:T(8,128)(2,1)S(1)} %all-to-all-done.x_ref.ids_ref, ...), custom_call_target="tpu_custom_call" | custom-call | flops 85899345920 | bytes 5111808 | tf_op jit(solution)/shard_map/attend_backward/pallas_call | solution.py:314
  394.3 6.0 all-to-all-start.7
  400.3 1.2 pad_add_fusion.info_ref
  401.5 41.9 %middle_part.3 = (bf16[2,1,512,1024]{3,2,1,0:T(8,128)(2,1)}, bf16[1024,512]{1,0:T(8,128)(2,1)}, bf16[4096,512]{1,0:T(8,128)(2,1)}, bf16[512,4096]{1,0:T(8,128)(2...) custom-call(s32[2]{0:T(128)} %pad_add_fusion.info_ref, ...), custom_call_target="tpu_custom_call", output_to_operand_aliasing={{0}: (9, {})} | custom-call | flops 25769803776 | bytes 33554432 | tf_op jit(solution)/shard_map/middle_part/pallas_call | solution.py:519
  443.4 6.4 all-to-all-start.8
  449.8 1.2 copy-done.18
  451.1 13.7 %down_grad.1.refs_4_ = bf16[32,4,32,3072]{3,2,1,0:T(8,128)(2,1)} custom-call(bf16[4096,512]{1,0:T(8,128)(2,1)} %get-tuple-element.140.refs_0_, bf16[4096,512]{1,0:T(8,128)(2,1)} %get-tuple-element.141.refs_1_, bf16[512,1024]{1,0:T(8,128)(2,1)S(1)} %copy-done.17, bf16[512,1024]{1,0:T(8,128)(2,1)S(1)} %copy-done.18), custom_call_target="tpu_custom_call" | custom-call | flops 8589934592 | bytes 8388608 | tf_op jit(solution)/shard_map/down_grad/pallas_call | solution.py:584
  464.8 13.6 %gate_grad.1.refs_4_ = bf16[32,4,32,3072]{3,2,1,0:T(8,128)(2,1)} custom-call(bf16[1024,512]{1,0:T(8,128)(2,1)S(1)} %copy-done.6, bf16[1024,512]{1,0:T(8,128)(2,1)S(1)} %copy-done.7, bf16[512,4096]{1,0:T(8,128)(2,1)} %get-tuple-element.138.refs_2_, bf16[512,4096]{1,0:T(8,128)(2,1)} %get-tuple-element.139.refs_3_, ...), custom_call_target="tpu_custom_call", output_to_operand_aliasing={{}: (4, {})} | custom-call | flops 8589934592 | bytes 8388608 | tf_op jit(solution)/shard_map/gate_grad/pallas_call | solution.py:584
  478.4 13.6 %up_grad.1 = bf16[32,4,32,3072]{3,2,1,0:T(8,128)(2,1)} custom-call(bf16[1024,512]{1,0:T(8,128)(2,1)S(1)} %copy-done.6, bf16[1024,512]{1,0:T(8,128)(2,1)S(1)} %copy-done.7, bf16[512,4096]{1,0:T(8,128)(2,1)} %get-tuple-element.136.refs_2_, bf16[512,4096]{1,0:T(8,128)(2,1)} %get-tuple-element.137.refs_3_, ...), custom_call_target="tpu_custom_call", output_to_operand_aliasing={{}: (4, {})} | custom-call | flops 8589934592 | bytes 8388608 | tf_op jit(solution)/shard_map/up_grad/pallas_call | solution.py:584
  492.0 50.0 %attend_backward.5 = (bf16[8,192,512]{2,1,0:T(8,128)(2,1)S(1)}, f32[8,128]{1,0:T(8,128)S(1)}) custom-call(s32[1]{0:T(128)} %bitcast.7.len_ref, f32[2,2]{1,0:T(2,128)S(1)} %copy.37.bias_ref, bf16[8,192,512]{2,1,0:T(8,128)(2,1)} %all-to-all-done.1.x_ref, bf16[8,208,512]{2,1,0:T(8,128)(2,1)} %copy-done.8, bf16[8,128,512]{2,1,0:T(8,128)(2,1)S(1)} %copy-done.23, ...), custom_call_target="tpu_custom_call" | custom-call | flops 85899345920 | bytes 4718592 | tf_op jit(solution)/shard_map/attend_backward/pallas_call | solution.py:314
  543.2 6.1 all-to-all-start.9
  549.3 11.8 %attend_backward.6 = (bf16[8,192,512]{2,1,0:T(8,128)(2,1)S(1)}, f32[8,128]{1,0:T(8,128)S(1)}) custom-call(s32[1]{0:T(128)} %bitcast.len_ref, f32[2,2]{1,0:T(2,128)S(1)} %copy.37.bias_ref, bf16[8,208,512]{2,1,0:T(8,128)(2,1)} %all-to-all-done.2.x_ref.ids_ref, bf16[8,208,512]{2,1,0:T(8,128)(2,1)} %all-to-all-done.2.x_ref.ids_ref, ...), custom_call_target="tpu_custom_call" | custom-call | flops 85899345920 | bytes 5111808 | tf_op jit(solution)/shard_map/attend_backward/pallas_call | solution.py:314
  562.2 23.0 %all-to-all-done.9.rest_1_ = bf16[8,192,512]{2,1,0:T(8,128)(2,1)} async-done(((bf16[8,192,512]{2,1,0:T(8,128)(2,1)}), bf16[8,192,512]{2,1,0:T(8,128)(2,1)}, u32[]{:S(2)}, u32[]{:S(2)}) %all-to-all-start.9) | async-done | bytes 1572896 | tf_op jit(solution)/shard_map/all_to_all | solution.py:757
  585.3 5.9 all-to-all-start.10
  591.1 11.7 %attend_backward.7 = (bf16[8,192,512]{2,1,0:T(8,128)(2,1)S(1)}, f32[8,128]{1,0:T(8,128)S(1)}) custom-call(s32[1]{0:T(128)} %bitcast.len_ref, f32[2,2]{1,0:T(2,128)S(1)} %copy.37.bias_ref, bf16[8,192,512]{2,1,0:T(8,128)(2,1)} %all-to-all-done.4.x_ref, bf16[8,208,512]{2,1,0:T(8,128)(2,1)} %all-to-all-done.2.x_ref.ids_ref, ...), custom_call_target="tpu_custom_call" | custom-call | flops 85899345920 | bytes 4718592 | tf_op jit(solution)/shard_map/attend_backward/pallas_call | solution.py:314
  604.0 9.2 all-to-all-done.10.rest_0_
  613.3 4.3 all-to-all-start.11
  617.7 10.2 final_part.2
  630.8 18.9 %all-to-all-done.11.rest_1_ = bf16[8,192,512]{2,1,0:T(8,128)(2,1)} async-done(((bf16[8,192,512]{2,1,0:T(8,128)(2,1)}), bf16[8,192,512]{2,1,0:T(8,128)(2,1)}, u32[]{:S(2)}, u32[]{:S(2)}) %all-to-all-start.11) | async-done | bytes 1572896 | tf_op jit(solution)/shard_map/all_to_all | solution.py:757
  649.7 10.6 final_part.3
  663.4 12.7 %attn_weight_grads.1 = (bf16[1024,1024]{1,0:T(8,128)(2,1)}, bf16[1024,1024]{1,0:T(8,128)(2,1)}, bf16[1024,1024]{1,0:T(8,128)(2,1)}, bf16[1024,1024]{1,0:T(8,128)(2,1)}) custom-call(bf16[1024,512]{1,0:T(8,128)(2,1)S(1)} %copy-done.39, bf16[1024,512]{1,0:T(8,128)(2,1)S(1)} %copy-done.41, bf16[1024,512]{1,0:T(8,128)(2,1)} %bitcast.8.mixed_ref.refs_2_, ...), custom_call_target="tpu_custom_call" | custom-call | flops 8589934592 | bytes 8388608 | tf_op jit(solution)/shard_map/attn_weight_grads/pallas_call | solution.py:723
  676.1 3.4 constant_dynamic-update-slice_fusion.3
  679.5 1.6 constant_dynamic-update-slice_fusion.2
  681.8 1.5 constant_dynamic-update-slice_fusion.1
  684.2 1.6 constant_dynamic-update-slice_fusion
  692.8 1.4 maximum_bitcast_fusion
  696.0 1.4 maximum_bitcast_fusion.2
  697.6 58.1 %all-reduce = (f32[1024]{0:T(1024)}, f32[16,2]{0,1:T(2,128)}, f32[1024]{0:T(1024)}) all-reduce(f32[1024]{0:T(1024)S(1)} %bitcast.60, f32[16,2]{0,1:T(2,128)S(1)} %dynamic_update_slice.3, f32[1024]{0:T(1024)S(1)} %bitcast.59), channel_id=1, replica_groups=mesh['shard'=4,'seq'=8] {'shard','seq'}, use_global_device_ids=true, to_apply=%region_0.0 | all-reduce | flops 2080 | bytes 16640 | tf_op jit(solution)/shard_map/psum | solution.py:961
  755.6 81.7 %reduce-scatter.3.cloned.1.call-done = bf16[32,4224]{1,0:T(8,128)(2,1)} async-done(((bf16[1024,4224]{1,0:T(8,128)(2,1)}), bf16[32,4224]{1,0:T(8,128)(2,1)}) %reduce-scatter.3.cloned.1.call-update) | async-done | bytes 270352 | tf_op jit(solution)/shard_map/reduce_scatter | solution.py:956
  837.3 1.7 fusion
  839.1 249.4 %reduce-scatter.5.cloned.1.call-done = bf16[128,3072]{1,0:T(8,128)(2,1)} async-done(((bf16[4096,3072]{1,0:T(8,128)(2,1)}), bf16[128,3072]{1,0:T(8,128)(2,1)}) %reduce-scatter.5.cloned.1.call-update) | async-done | bytes 786448 | tf_op jit(solution)/shard_map/reduce_scatter | solution.py:947
  1088.5 2.0 slice_convert_fusion
  (147 shorter events, 27.8 us)
Async XLA Ops:
  7.2 73.5 %copy-start = (f32[16,2]{0,1:T(2,128)S(1)}, f32[16,2]{0,1:T(2,128)}, u32[]{:S(2)}) copy-start(f32[16,2]{0,1:T(2,128)} %param.25) | copy-start | bytes 388
  7.2 52.1 %all-gather.6.cloned.1.call-start = ((), (), s32[]{:S(2)}) async-start(), calls=%async_computation.14 | async-start | bytes 7864320 | tf_op jit(solution)/shard_map/all_gather | solution.py:754
  9.9 231.0 %all-gather.8.cloned.1.call-start = ((), (), s32[]{:S(2)}) async-start(), calls=%async_computation.15 | async-start | bytes 2621440 | tf_op jit(solution)/shard_map/all_gather | solution.py:754
  10.6 1.3 copy-start.54
  10.6 1.4 copy-start.55
  10.7 48.6 %copy-start.36 = (f32[1024]{0:T(1024)S(1)}, f32[1024]{0:T(1024)}, u32[]{:S(2)}) copy-start(f32[1024]{0:T(1024)} %param.20) | copy-start | bytes 12292
  10.7 230.2 %all-gather.10.cloned.1.call-start = ((), (), s32[]{:S(2)}) async-start(), calls=%async_computation.16 | async-start | bytes 10485760 | tf_op jit(solution)/shard_map/all_gather | solution.py:754
  11.4 229.5 %all-gather.12.cloned.1.call-start = ((), (), s32[]{:S(2)}) async-start(), calls=%async_computation.17 | async-start | bytes 10485760 | tf_op jit(solution)/shard_map/all_gather | solution.py:754
  12.6 58.5 %copy-start.32 = (f32[32,512]{1,0:T(8,128)}, f32[32,512]{1,0:T(8,128)S(1)}, u32[]{:S(2)}) copy-start(f32[32,512]{1,0:T(8,128)S(1)} %get-tuple-element.197.sin_ref) | copy-start | bytes 196612
  12.6 58.5 %copy-start.34 = (f32[32,512]{1,0:T(8,128)}, f32[32,512]{1,0:T(8,128)S(1)}, u32[]{:S(2)}) copy-start(f32[32,512]{1,0:T(8,128)S(1)} %get-tuple-element.198.cos_ref) | copy-start | bytes 196612
  12.6 68.9 %copy-start.28 = (f32[32,512]{1,0:T(8,128)}, f32[32,512]{1,0:T(8,128)S(1)}, u32[]{:S(2)}) copy-start(f32[32,512]{1,0:T(8,128)S(1)} %get-tuple-element.203.cos_ref) | copy-start | bytes 196612
  12.6 68.8 %copy-start.30 = (f32[32,512]{1,0:T(8,128)}, f32[32,512]{1,0:T(8,128)S(1)}, u32[]{:S(2)}) copy-start(f32[32,512]{1,0:T(8,128)S(1)} %get-tuple-element.204.sin_ref) | copy-start | bytes 196612
  59.3 2.8 copy-start.2
  62.1 1.6 copy-start.4
  71.1 1.2 copy-start.9
  72.3 1.2 copy-start.12
  74.5 6.4 copy-start.56
  74.5 45.9 %all-to-all-start = ((bf16[8,208,512]{2,1,0:T(8,128)(2,1)}), bf16[8,208,512]{2,1,0:T(8,128)(2,1)S(1)}, u32[]{:S(2)}, u32[]{:S(2)}) async-start(bf16[8,208,512]{2,1,0:T(8,128)(2,1)} %copy-done.9), calls=%async_computation | async-start | bytes 3407872 | tf_op jit(solution)/shard_map/all_to_all | solution.py:757
  80.1 182.8 %all-gather.14.cloned.1.call-start = ((), (), s32[]{:S(2)}) async-start(), calls=%async_computation.18 | async-start | bytes 10485760 | tf_op jit(solution)/shard_map/all_gather | solution.py:754
  81.5 2.8 copy-start.3
  84.3 1.6 copy-start.5
  93.3 1.2 copy-start.10
  95.6 54.9 %copy-start.40 = (bf16[1024,512]{1,0:T(8,128)(2,1)}, bf16[1024,512]{1,0:T(8,128)(2,1)S(1)}, u32[]{:S(2)}) copy-start(bf16[1024,512]{1,0:T(8,128)(2,1)S(1)} %get-tuple-element.100.refs_1_) | copy-start | bytes 3145732
  120.3 221.1 %copy-start.8 = (bf16[8,208,512]{2,1,0:T(8,128)(2,1)}, bf16[8,208,512]{2,1,0:T(8,128)(2,1)S(1)}, u32[]{:S(2)}) copy-start(bf16[8,208,512]{2,1,0:T(8,128)(2,1)S(1)} %all-to-all-done.x_ref.ids_ref) | copy-start | bytes 5111812
  120.3 40.9 %all-to-all-start.1 = ((bf16[8,192,512]{2,1,0:T(8,128)(2,1)}), bf16[8,192,512]{2,1,0:T(8,128)(2,1)}, u32[]{:S(2)}, u32[]{:S(2)}) async-start(bf16[8,192,512]{2,1,0:T(8,128)(2,1)} %copy-done.12), calls=%async_computation.1 | async-start | bytes 3145728 | tf_op jit(solution)/shard_map/all_to_all | solution.py:757
  161.3 43.7 %all-to-all-start.2 = ((bf16[8,208,512]{2,1,0:T(8,128)(2,1)}), bf16[8,208,512]{2,1,0:T(8,128)(2,1)}, u32[]{:S(2)}, u32[]{:S(2)}) async-start(bf16[8,208,512]{2,1,0:T(8,128)(2,1)} %copy-done.10), calls=%async_computation.2 | async-start | bytes 3407872 | tf_op jit(solution)/shard_map/all_to_all | solution.py:757
  205.0 29.9 %all-to-all-start.3 = ((bf16[8,128,512]{2,1,0:T(8,128)(2,1)}), bf16[8,128,512]{2,1,0:T(8,128)(2,1)}, u32[]{:S(2)}, u32[]{:S(2)}) async-start(bf16[8,128,512]{2,1,0:T(8,128)(2,1)} %get-tuple-element.110.mixed_ref), calls=%async_computation.3 | async-start | bytes 2097152 | tf_op jit(solution)/shard_map/all_to_all | solution.py:757
  234.9 69.9 %all-to-all-start.4 = ((bf16[8,192,512]{2,1,0:T(8,128)(2,1)}), bf16[8,192,512]{2,1,0:T(8,128)(2,1)}, u32[]{:S(2)}, u32[]{:S(2)}) async-start(bf16[8,192,512]{2,1,0:T(8,128)(2,1)} %copy-done.11), calls=%async_computation.4 | async-start | bytes 3145728 | tf_op jit(solution)/shard_map/all_to_all | solution.py:757
  304.8 31.7 %all-to-all-start.5 = ((bf16[8,128,512]{2,1,0:T(8,128)(2,1)}), bf16[8,128,512]{2,1,0:T(8,128)(2,1)S(1)}, u32[]{:S(2)}, u32[]{:S(2)}) async-start(bf16[8,128,512]{2,1,0:T(8,128)(2,1)} %bitcast.56), calls=%async_computation.5 | async-start | bytes 2097152 | tf_op jit(solution)/shard_map/all_to_all | solution.py:757
  310.3 1.2 copy-start.25
  337.6 55.8 %all-to-all-start.6 = ((bf16[8,128,512]{2,1,0:T(8,128)(2,1)}), bf16[8,128,512]{2,1,0:T(8,128)(2,1)S(1)}, u32[]{:S(2)}, u32[]{:S(2)}) async-start(bf16[8,128,512]{2,1,0:T(8,128)(2,1)} %copy-done.26), calls=%async_computation.6 | async-start | bytes 2097152 | tf_op jit(solution)/shard_map/all_to_all | solution.py:757
  341.4 1.2 copy-start.22
  392.2 1.1 copy-start.14
  394.3 49.1 %all-to-all-start.7 = ((bf16[8,192,512]{2,1,0:T(8,128)(2,1)}), bf16[8,192,512]{2,1,0:T(8,128)(2,1)S(1)}, u32[]{:S(2)}, u32[]{:S(2)}) async-start(bf16[8,192,512]{2,1,0:T(8,128)(2,1)} %copy-done.14), calls=%async_computation.7 | async-start | bytes 3145728 | tf_op jit(solution)/shard_map/all_to_all | solution.py:757
  443.4 6.4 copy-start.17
  443.4 48.6 %all-to-all-start.8 = ((bf16[8,128,512]{2,1,0:T(8,128)(2,1)}), bf16[8,128,512]{2,1,0:T(8,128)(2,1)}, u32[]{:S(2)}, u32[]{:S(2)}) async-start(bf16[8,128,512]{2,1,0:T(8,128)(2,1)} %bitcast.55), calls=%async_computation.8 | async-start | bytes 2097152 | tf_op jit(solution)/shard_map/all_to_all | solution.py:757
  449.8 1.2 copy-start.18
  451.1 13.7 %copy-start.6 = (bf16[1024,512]{1,0:T(8,128)(2,1)S(1)}, bf16[1024,512]{1,0:T(8,128)(2,1)}, u32[]{:S(2)}) copy-start(bf16[1024,512]{1,0:T(8,128)(2,1)} %get-tuple-element.134.refs_0_) | copy-start | bytes 3145732
  451.1 13.7 %copy-start.7 = (bf16[1024,512]{1,0:T(8,128)(2,1)S(1)}, bf16[1024,512]{1,0:T(8,128)(2,1)}, u32[]{:S(2)}) copy-start(bf16[1024,512]{1,0:T(8,128)(2,1)} %get-tuple-element.135.refs_1_) | copy-start | bytes 3145732
  478.4 13.6 %copy-start.23 = (bf16[8,128,512]{2,1,0:T(8,128)(2,1)S(1)}, bf16[8,128,512]{2,1,0:T(8,128)(2,1)}, u32[]{:S(2)}) copy-start(bf16[8,128,512]{2,1,0:T(8,128)(2,1)} %copy-done.21) | copy-start | bytes 3145732
  542.0 1.1 copy-start.16
  543.2 6.1 copy-start.27
  543.2 42.1 %all-to-all-start.9 = ((bf16[8,192,512]{2,1,0:T(8,128)(2,1)}), bf16[8,192,512]{2,1,0:T(8,128)(2,1)}, u32[]{:S(2)}, u32[]{:S(2)}) async-start(bf16[8,192,512]{2,1,0:T(8,128)(2,1)} %copy-done.16), calls=%async_computation.9 | async-start | bytes 3145728 | tf_op jit(solution)/shard_map/all_to_all | solution.py:757
  561.1 1.1 copy-start.15
  585.3 28.0 %all-to-all-start.10 = ((bf16[8,192,512]{2,1,0:T(8,128)(2,1)}), bf16[8,192,512]{2,1,0:T(8,128)(2,1)}, u32[]{:S(2)}, u32[]{:S(2)}) async-start(bf16[8,192,512]{2,1,0:T(8,128)(2,1)} %copy-done.15), calls=%async_computation.10 | async-start | bytes 3145728 | tf_op jit(solution)/shard_map/all_to_all | solution.py:757
  602.9 1.2 copy-start.13
  604.0 13.6 %copy-start.33 = (f32[32,512]{1,0:T(8,128)S(1)}, f32[32,512]{1,0:T(8,128)}, u32[]{:S(2)}) copy-start(f32[32,512]{1,0:T(8,128)} %copy-done.32) | copy-start | bytes 196612
  604.0 13.6 %copy-start.35 = (f32[32,512]{1,0:T(8,128)S(1)}, f32[32,512]{1,0:T(8,128)}, u32[]{:S(2)}) copy-start(f32[32,512]{1,0:T(8,128)} %copy-done.34) | copy-start | bytes 196612
  604.0 13.6 %copy-start.37 = (f32[1024]{0:T(1024)S(1)}, f32[1024]{0:T(1024)}, u32[]{:S(2)}) copy-start(f32[1024]{0:T(1024)} %param.20) | copy-start | bytes 12292
  613.3 36.4 %all-to-all-start.11 = ((bf16[8,192,512]{2,1,0:T(8,128)(2,1)}), bf16[8,192,512]{2,1,0:T(8,128)(2,1)}, u32[]{:S(2)}, u32[]{:S(2)}) async-start(bf16[8,192,512]{2,1,0:T(8,128)(2,1)} %copy-done.13), calls=%async_computation.11 | async-start | bytes 3145728 | tf_op jit(solution)/shard_map/all_to_all | solution.py:757
  617.6 219.8 %reduce-scatter.3.cloned.1.call-start = ((), (), s32[]{:S(2)}) async-start(), calls=%async_computation.19 | async-start | bytes 8921088 | tf_op jit(solution)/shard_map/reduce_scatter | solution.py:956
  617.6 32.1 %copy-start.29 = (f32[32,512]{1,0:T(8,128)S(1)}, f32[32,512]{1,0:T(8,128)}, u32[]{:S(2)}) copy-start(f32[32,512]{1,0:T(8,128)} %copy-done.28) | copy-start | bytes 196612
  617.6 32.1 %copy-start.31 = (f32[32,512]{1,0:T(8,128)S(1)}, f32[32,512]{1,0:T(8,128)}, u32[]{:S(2)}) copy-start(f32[32,512]{1,0:T(8,128)} %copy-done.30) | copy-start | bytes 196612
  649.7 13.6 %copy-start.20 = (bf16[8,128,512]{2,1,0:T(8,128)(2,1)S(1)}, bf16[8,128,512]{2,1,0:T(8,128)(2,1)}, u32[]{:S(2)}) copy-start(bf16[8,128,512]{2,1,0:T(8,128)(2,1)} %copy-done.19) | copy-start | bytes 3145732
  649.7 13.6 %copy-start.39 = (bf16[1024,512]{1,0:T(8,128)(2,1)S(1)}, bf16[1024,512]{1,0:T(8,128)(2,1)}, u32[]{:S(2)}) copy-start(bf16[1024,512]{1,0:T(8,128)(2,1)} %copy-done.38) | copy-start | bytes 3145732
  649.7 13.6 %copy-start.41 = (bf16[1024,512]{1,0:T(8,128)(2,1)S(1)}, bf16[1024,512]{1,0:T(8,128)(2,1)}, u32[]{:S(2)}) copy-start(bf16[1024,512]{1,0:T(8,128)(2,1)} %copy-done.40) | copy-start | bytes 3145732
  649.7 13.6 %copy-start.43 = (bf16[1024,512]{1,0:T(8,128)(2,1)S(1)}, bf16[1024,512]{1,0:T(8,128)(2,1)}, u32[]{:S(2)}) copy-start(bf16[1024,512]{1,0:T(8,128)(2,1)} %copy-done.42) | copy-start | bytes 3145732
  676.0 3.4 copy-start.51
  679.5 2.3 copy-start.50
  681.8 2.3 copy-start.49
  686.5 2.6 copy-start.52
  686.5 2.6 copy-start.53
  686.5 402.0 %reduce-scatter.5.cloned.1.call-start = ((), (), s32[]{:S(2)}) async-start(), calls=%async_computation.20 | async-start | bytes 25952256 | tf_op jit(solution)/shard_map/reduce_scatter | solution.py:947
  1088.5 3.8 copy-start.1
  (12 other events, 12.0 us)
Sparse Core Ops, SparseCore 0:
  10.2 49.0 all-gather.5
  60.8 22.5 all-gather.7
  85.0 58.2 all-gather.9
  144.8 58.2 all-gather.11
  204.5 58.3 all-gather.13
  686.6 150.6 reduce-scatter.2
  843.8 244.7 reduce-scatter.4
